TPU v7x, 128 devices: a whole 4x4x4 slice. The times are simulated.
128 devices in a mesh: gy: 8 (over x_hi, y), gx: 16 (over z, x_lo, core).
Axes of the slice: x: 4 (x_hi: 2, x_lo: 2; x = x_hi * 2 + x_lo), y: 4, z: 4, core: 2. Of those that a mesh axis runs over, the one named last changes fastest.
Arguments:
- features: bfloat16 [256, 2048, 256], P('gy', 'gx'), may hold values from -8 to 8
- tissue: int32 [16, 128], P('gy', 'gx'), may hold values 0 or 1
- owner_map: int32 [8, 16, 16, 1], P('gy', 'gx'), may hold values from 0 to 15; in each aligned block of 16 rows (0 to 15, 16 to 31, ..., all dimensions but the last counted through in order) at most 2 rows name the same one
- w_conv: bfloat16 [9, 256, 256], replicated, may hold values from -0.125 to 0.125
- w_stride: bfloat16 [4, 256, 256], replicated, may hold values from -0.1875 to 0.1875
- w_query: float32 [256, 256], replicated, may hold values from -0.375 to 0.375
- w_key: float32 [256, 256], replicated, may hold values from -0.375 to 0.375
- w_value: float32 [256, 256], replicated, may hold values from -0.375 to 0.375
- cotangent: float32 [256], replicated, may hold values from -6 to 6
Outputs:
- embedding: float32 [256], replicated
- input_grad: bfloat16 [256, 2048, 256], P('gy', 'gx')
- conv_grad: float32 [9, 256, 256], replicated
Inputs may be any that keep to these rules, and one draw needn't show every extreme that they name: `owner_map`: among the tiles of one device, no owner index is named more than 2 times.
All inputs are finite; a program needn't handle non-finite values. No bound on the sum of `tissue` on one device may be relied on, other than what follows from the above.
Results may differ from a plain program's by a relative error of at most 0.017.
Values may be sent and summed in bfloat16 or wider, within the bound.
A program may use at most 128 MiB of HBM per device.

v0:
```python
from functools import partial
import math

import jax
import jax.numpy as jnp
from jax import lax
from jax.sharding import PartitionSpec as P

HEADS = 4
CAP = 2


attention_bias = -1.0
loss_scale = 512.0


def extended(block, sides, width):
    for axis, dim in sides:
        count = lax.axis_size(axis)
        forward = [(i, i + 1) for i in range(count - 1)]
        backward = [(target, source) for source, target in forward]
        low = lax.ppermute(
            lax.slice_in_dim(block, block.shape[dim] - width, None, axis=dim), axis, forward
        )
        high = lax.ppermute(lax.slice_in_dim(block, 0, width, axis=dim), axis, backward)
        block = jnp.concatenate([low, block, high], axis=dim)
    return block


def forward_taps(padded, weight, pix_rows, pix_cols):
    channels = padded.shape[2]
    running = jnp.zeros((pix_rows * pix_cols, weight.shape[2]), jnp.float32)
    for tap_index in range(9):
        row_off, col_off = (tap_index // 3, tap_index % 3)
        window = padded[row_off : row_off + pix_rows, col_off : col_off + pix_cols].reshape(
            pix_rows * pix_cols, channels
        )
        running = running + jnp.dot(window, weight[tap_index], preferred_element_type=jnp.float32)
    return running.reshape(pix_rows, pix_cols, weight.shape[2])


def backward_taps(padded, weight, pix_rows, pix_cols):
    channels = padded.shape[2]
    running = jnp.zeros((pix_rows * pix_cols, weight.shape[1]), jnp.float32)
    for tap_index in range(9):
        row_off, col_off = (tap_index // 3, tap_index % 3)
        window = padded[
            2 - row_off : 2 - row_off + pix_rows, 2 - col_off : 2 - col_off + pix_cols
        ].reshape(pix_rows * pix_cols, channels)
        running = running + lax.dot_general(
            window, weight[tap_index], (((1,), (1,)), ((), ())), preferred_element_type=jnp.float32
        )
    return running.reshape(pix_rows, pix_cols, weight.shape[1])


def weight_taps(padded, upstream, pix_rows, pix_cols):
    channels = padded.shape[2]
    flat_up = upstream.reshape(pix_rows * pix_cols, upstream.shape[2])
    pieces = []
    for tap_index in range(9):
        row_off, col_off = (tap_index // 3, tap_index % 3)
        window = padded[row_off : row_off + pix_rows, col_off : col_off + pix_cols].reshape(
            pix_rows * pix_cols, channels
        )
        pieces.append(
            lax.dot_general(
                window, flat_up, (((0,), (0,)), ((), ())), preferred_element_type=jnp.float32
            )
        )
    return jnp.stack(pieces)


def strided_forward(field, weight):
    pix_rows, pix_cols, channels = field.shape
    running = jnp.zeros((pix_rows // 2 * (pix_cols // 2), weight.shape[2]), jnp.float32)
    for tap_index in range(4):
        row_off, col_off = (tap_index // 2, tap_index % 2)
        window = field[row_off::2, col_off::2].reshape(-1, channels)
        running = running + jnp.dot(window, weight[tap_index], preferred_element_type=jnp.float32)
    return running.reshape(pix_rows // 2, pix_cols // 2, weight.shape[2])


def strided_backward(upstream, weight):
    half_rows, half_cols, channels = upstream.shape
    flat_up = upstream.reshape(half_rows * half_cols, channels)
    tap_parts = []
    for tap_index in range(4):
        tap_parts.append(
            lax.dot_general(
                flat_up,
                weight[tap_index],
                (((1,), (1,)), ((), ())),
                preferred_element_type=jnp.float32,
            ).reshape(half_rows, half_cols, -1)
        )
    upper_rows = jnp.stack([tap_parts[0], tap_parts[1]], axis=2)
    bottom = jnp.stack([tap_parts[2], tap_parts[3]], axis=2)
    stacked = jnp.stack([upper_rows, bottom], axis=1)
    return stacked.reshape(2 * half_rows, 2 * half_cols, -1)


def rms_normed(tokens_in):
    return tokens_in * lax.rsqrt(jnp.mean(tokens_in * tokens_in, axis=-1, keepdims=True) + 1e-05)


def silu_slope(values):
    gate_sig = jax.nn.sigmoid(values)
    return gate_sig * (1.0 + values * (1.0 - gate_sig))


def attend(
    query_tokens,
    query_flags,
    query_groups,
    key_tokens,
    key_flags,
    key_groups,
    w_query,
    w_key,
    w_value,
    head_count,
):
    highest = lax.Precision.HIGHEST
    query_count = query_tokens.shape[0]
    key_count = key_tokens.shape[0]
    query_rows = jnp.dot(query_tokens, w_query, precision=highest).reshape(
        query_count, head_count, -1
    )
    key_rows = jnp.dot(key_tokens, w_key, precision=highest).reshape(key_count, head_count, -1)
    value_rows = jnp.dot(key_tokens, w_value, precision=highest).reshape(key_count, head_count, -1)
    scores = jnp.einsum("qhd,khd->hqk", query_rows, key_rows, precision=highest) / math.sqrt(
        query_rows.shape[2]
    )
    allowed = (query_groups[:, None] == key_groups[None, :]).astype(jnp.float32) * key_flags[
        None, :
    ]
    weights = jax.nn.sigmoid(scores + attention_bias) * allowed[None]
    mixed_rows = jnp.einsum("hqk,khd->qhd", weights, value_rows, precision=highest).reshape(
        query_count, -1
    )
    return jnp.dot(query_flags, mixed_rows, precision=highest)


def self_attend(tokens_in, tile_flags, tile_groups, w_query, w_key, w_value, head_count):
    return attend(
        tokens_in,
        tile_flags,
        tile_groups,
        tokens_in,
        tile_flags,
        tile_groups,
        w_query,
        w_key,
        w_value,
        head_count,
    )


def per_device(features, tissue, owner_map, w_conv, w_stride, w_query, w_key, w_value, cotangent):
    pix_rows, pix_cols, channels = features.shape
    tile_rows, tile_cols = tissue.shape
    cell_side = pix_rows // (2 * tile_rows)
    gx_count = lax.axis_size("gx")
    tiles_all = tile_rows * tile_cols * lax.axis_size("gy") * gx_count
    norm_scale = 1.0 / math.sqrt(tiles_all)
    seed_grad = cotangent * (loss_scale * norm_scale)
    padded = extended(features, (("gy", 0), ("gx", 1)), 1)
    pre_act = forward_taps(padded, w_conv, pix_rows, pix_cols)
    pixel_mask = jnp.repeat(
        jnp.repeat(tissue.astype(jnp.float32), 2 * cell_side, axis=0), 2 * cell_side, axis=1
    )[:, :, None]
    summed = (features.astype(jnp.float32) + jax.nn.silu(pre_act) * pixel_mask).astype(jnp.bfloat16)
    reduced = strided_forward(summed, w_stride)
    pooled = (
        reduced.reshape(tile_rows, cell_side, tile_cols, cell_side, channels)
        .mean(axis=(1, 3))
        .reshape(-1, channels)
    )
    normed = rms_normed(pooled).astype(jnp.bfloat16)
    tile_flags = tissue.reshape(-1).astype(jnp.float32)
    owners = owner_map.reshape(-1)
    slot_count = gx_count * CAP
    choose = (owners[:, None] == jnp.arange(gx_count, dtype=jnp.int32)[None, :]).astype(jnp.int32)
    earlier = jnp.cumsum(choose, axis=0) - choose
    rank_in = jnp.sum(earlier * choose, axis=1)
    slot_of = owners * CAP + rank_in
    slot_place = (jnp.arange(slot_count, dtype=jnp.int32)[:, None] == slot_of[None, :]).astype(
        jnp.bfloat16
    )
    sent_tokens = (
        jnp.dot(slot_place, normed, preferred_element_type=jnp.float32)
        .astype(jnp.bfloat16)
        .reshape(gx_count, CAP, channels)
    )
    sent_flags = (
        jnp.dot(slot_place, tile_flags.astype(jnp.bfloat16), preferred_element_type=jnp.float32)
        .astype(jnp.bfloat16)
        .reshape(gx_count, CAP)
    )
    got_tokens, got_flags = (
        lax.all_to_all(sent_tokens, "gx", split_axis=0, concat_axis=0, tiled=True),
        lax.all_to_all(sent_flags, "gx", split_axis=0, concat_axis=0, tiled=True),
    )
    group_tokens = got_tokens.reshape(slot_count, channels).astype(jnp.float32)
    group_flags = got_flags.reshape(slot_count).astype(jnp.float32)
    group_ids = jnp.zeros((slot_count,), jnp.int32)
    group_fn = partial(
        self_attend,
        tile_flags=group_flags,
        tile_groups=group_ids,
        w_query=w_query,
        w_key=w_key,
        w_value=w_value,
        head_count=HEADS,
    )
    partial_sum, pull_group = jax.vjp(group_fn, group_tokens)
    slot_grads = pull_group(seed_grad)[0].astype(jnp.bfloat16).reshape(gx_count, CAP, channels)
    returned = lax.all_to_all(slot_grads, "gx", split_axis=0, concat_axis=0, tiled=True)
    token_grad = lax.dot_general(
        slot_place,
        returned.reshape(slot_count, channels),
        (((0,), (0,)), ((), ())),
        preferred_element_type=jnp.float32,
    )
    embedding = lax.psum(partial_sum, ("gy", "gx")) * norm_scale
    pooled_grad = jax.vjp(rms_normed, pooled)[1](token_grad)[0]
    cell_grad = (
        (pooled_grad / (cell_side * cell_side))
        .astype(jnp.bfloat16)
        .reshape(tile_rows, 1, tile_cols, 1, channels)
    )
    cell_grad = jnp.broadcast_to(
        cell_grad, (tile_rows, cell_side, tile_cols, cell_side, channels)
    ).reshape(pix_rows // 2, pix_cols // 2, channels)
    sum_grad = strided_backward(cell_grad, w_stride)
    pre_grad = (sum_grad * pixel_mask * silu_slope(pre_act)).astype(jnp.bfloat16)
    local_grads = weight_taps(padded, pre_grad, pix_rows, pix_cols)
    grad_pad = extended(pre_grad, (("gy", 0), ("gx", 1)), 1)
    input_grad = (sum_grad + backward_taps(grad_pad, w_conv, pix_rows, pix_cols)).astype(
        jnp.bfloat16
    )
    conv_grad = lax.psum(local_grads, ("gy", "gx"))
    conv_grad = conv_grad / loss_scale
    return (embedding, input_grad, conv_grad)


def solution(mesh):
    in_specs = (
        P("gy", "gx", None),
        P("gy", "gx"),
        P("gy", "gx", None, None),
        P(),
        P(),
        P(),
        P(),
        P(),
        P(),
    )
    out_specs = (P(), P("gy", "gx", None), P())
    return jax.shard_map(
        per_device, mesh=mesh, in_specs=in_specs, out_specs=out_specs, check_vma=False
    )
```

profile of v0, /device:TPU:1, one launch (start us, length us, event | category | flops | bytes accessed | tf_op | source)
XLA Modules:
  0.0 436.3 jit_solution(15999486301501065111)
XLA Ops:
  7.2 3.2 copy.54
  10.4 4.0 collective-permute-start
  17.0 7.2 %all-to-all-start = ((bf16[16,1,2]{2,1,0:T(2,128)(2,1)}), bf16[16,1,2]{2,1,0:T(2,128)(2,1)}, u32[]{:S(2)}, u32[]{:S(2)}) async-start(bf16[16,1,2]{2,1,0:T(2,128)(2,1)} %all_to_all.16), calls=%async_computation | async-start | bytes 16384 | tf_op jit(solution)/shard_map/all_to_all | solution.py:202
  25.3 3.0 fusion.131
  32.7 3.5 collective-permute-start.2
  41.0 4.1 copy.69
  45.0 4.1 copy.61
  52.9 7.1 %pad_maximum_fusion = (bf16[34,129,256]{1,2,0:T(8,128)(2,1)S(1)}, bf16[34,129,256]{1,2,0:T(8,128)(2,1)}) fusion(bf16[34,1,256]{1,2,0:T(8,128)(2,1)} %copy.63, bf16[1,128,256]{1,2,0:T(8,128)(2,1)S(1)} %collective-permute-done.1, bf16[32,128,256]{1,2,0:T(8,128)(2,1)S(1)} %copy.54, bf16[1,128,256]{1,2,0:T(8,128)(2,1)S(1)} %collective-permute-done, ...), kind=kLoop, calls=%fused_computation.17 | loop fusion | flops 17965056 | bytes 6754304 | tf_op jit(solution)/shard_map/concatenate | solution.py:26
  60.0 3.6 fusion.127
  63.6 4.1 copy.70
  67.7 4.1 copy.66
  71.8 2.9 copy.64
  74.7 5.8 %fusion.128 = (bf16[32,128,256]{1,2,0:T(8,128)(2,1)}, bf16[32,128,256]{1,2,0:T(8,128)(2,1)S(1)}, bf16[32,128,256]{1,2,0:T(8,128)(2,1)}) fusion(bf16[34,129,256]{1,2,0:T(8,128)(2,1)} %get-tuple-element.20), kind=kLoop, calls=%fused_computation.195 | loop fusion | bytes 12582912 | tf_op jit(solution)/shard_map/slice | solution.py:35
  80.4 4.1 copy.67
  84.5 2.9 copy.65
  87.4 3.4 copy.59
  108.0 5.3 %slice.187 = bf16[16,64,256]{2,1,0:T(8,128)(2,1)} slice(bf16[32,128,256]{2,1,0:T(8,128)(2,1)S(1)} %add_convert_fusion.1), slice={[1:32:2], [1:128:2], [0:256:1]} | slice | bytes 1048576 | tf_op jit(solution)/shard_map/slice | solution.py:78
  113.3 5.3 %slice.185 = bf16[16,64,256]{2,1,0:T(8,128)(2,1)} slice(bf16[32,128,256]{2,1,0:T(8,128)(2,1)S(1)} %add_convert_fusion.1), slice={[1:32:2], [0:128:2], [0:256:1]} | slice | bytes 1048576 | tf_op jit(solution)/shard_map/slice | solution.py:78
  118.5 5.3 %slice.183 = bf16[16,64,256]{2,1,0:T(8,128)(2,1)} slice(bf16[32,128,256]{2,1,0:T(8,128)(2,1)S(1)} %add_convert_fusion.1), slice={[0:32:2], [1:128:2], [0:256:1]} | slice | bytes 1048576 | tf_op jit(solution)/shard_map/slice | solution.py:78
  123.8 5.3 %slice.181 = bf16[16,64,256]{2,1,0:T(8,128)(2,1)} slice(bf16[32,128,256]{2,1,0:T(8,128)(2,1)S(1)} %add_convert_fusion.1), slice={[0:32:2], [0:128:2], [0:256:1]} | slice | bytes 1048576 | tf_op jit(solution)/shard_map/slice | solution.py:78
  134.4 5.8 %all-to-all-start.1 = ((bf16[16,2,256]{2,1,0:T(2,128)(2,1)}), bf16[16,2,256]{2,1,0:T(2,128)(2,1)S(1)}, u32[]{:S(2)}, u32[]{:S(2)}) async-start(bf16[16,2,256]{2,1,0:T(2,128)(2,1)} %reshape.228), calls=%async_computation.1 | async-start | bytes 32768 | tf_op jit(solution)/shard_map/all_to_all | solution.py:201
  149.3 68.0 %psum.14 = f32[256]{0:T(256)S(1)} all-reduce(f32[256]{0:T(256)S(1)} %bitcast.295), channel_id=1, replica_groups=mesh['gy'=8,'gx'=16] {'gy','gx'}, use_global_device_ids=true, to_apply=%region_4.5 | all-reduce | flops 256 | bytes 2048 | tf_op jit(solution)/shard_map/psum | solution.py:225
  218.9 4.0 all-to-all-start.2
  223.5 5.2 %all-to-all-done.2 = bf16[16,2,256]{2,1,0:T(2,128)(2,1)S(1)} async-done(((bf16[16,2,256]{2,1,0:T(2,128)(2,1)}), bf16[16,2,256]{2,1,0:T(2,128)(2,1)S(1)}, u32[]{:S(2)}, u32[]{:S(2)}) %all-to-all-start.2) | async-done | bytes 16416 | tf_op jit(solution)/shard_map/all_to_all | solution.py:218
  231.3 5.2 %copy.82 = f32[16,2,64,2,256]{4,3,2,1,0:T(2,128)} copy(f32[16,2,64,2,256]{4,2,0,3,1:T(8,128)S(1)} %pad_maximum_fusion.1) | data formatting | bytes 8388608 | tf_op jit(solution)/shard_map/stack | solution.py:98
  236.5 6.2 %reshape.236 = f32[32,128,256]{2,1,0:T(8,128)} reshape(f32[16,2,64,2,256]{4,3,2,1,0:T(2,128)} %copy.82) | data formatting | bytes 8388608 | tf_op jit(solution)/shard_map/reshape | solution.py:99
  242.7 4.3 multiply_convert_fusion.1
  247.1 3.2 fusion.29
  266.6 6.1 %reshape.241 = f32[4096,256]{1,0:T(8,128)} reshape(f32[16,2,64,2,256]{4,3,2,1,0:T(2,128)} %copy.82) | data formatting | bytes 8388608 | tf_op jit(solution)/shard_map/reshape | solution.py:99
  275.3 3.0 collective-permute-start.7
  296.7 129.2 %all-reduce.2.cloned.1.call-done = f32[9,256,256]{2,1,0:T(8,128)} async-done(((f32[9,256,256]{2,1,0:T(8,128)}), f32[9,256,256]{2,1,0:T(8,128)}) %all-reduce.2.cloned.1.call-update) | async-done | bytes 2359312 | tf_op jit(solution)/shard_map/psum | solution.py:242
  425.9 3.3 broadcast_multiply_fusion
  (205 shorter events, 89.6 us)
Async XLA Ops:
  7.2 8.6 %copy-start.31 = (s32[2,8]{1,0:T(2,128)S(1)}, s32[2,8]{1,0:T(2,128)}, u32[]{:S(2)}) copy-start(s32[2,8]{1,0:T(2,128)} %param.10) | copy-start | bytes 196
  7.2 8.7 %copy-start.30 = (s32[1,1,16,1]{2,3,1,0:T(1,128)S(1)}, s32[1,1,16,1]{2,3,1,0:T(1,128)}, u32[]{:S(2)}) copy-start(s32[1,1,16,1]{2,3,1,0:T(1,128)} %param.11) | copy-start | bytes 196
  10.4 42.5 %copy-start.3 = (bf16[32,128,256]{1,2,0:T(8,128)(2,1)}, bf16[32,128,256]{1,2,0:T(8,128)(2,1)S(1)}, u32[]{:S(2)}) copy-start(bf16[32,128,256]{1,2,0:T(8,128)(2,1)S(1)} %copy.54) | copy-start | bytes 6291460
  10.4 14.5 %collective-permute-start = (bf16[1,128,256]{1,2,0:T(8,128)(2,1)S(1)}, bf16[1,128,256]{1,2,0:T(8,128)(2,1)S(1)}, u32[]{:S(2)}, u32[]{:S(2)}) collective-permute-start(bf16[1,128,256]{1,2,0:T(8,128)(2,1)S(1)} %get-tuple-element.29), channel_id=1, source_target_pairs={{0,16},{16,32},{32,48},{48,64},{64,80},{80,96},{96,112},{1,17},{17... | collective-permute-start | bytes 196616 | tf_op jit(solution)/shard_map/ppermute | solution.py:22
  14.5 10.5 %collective-permute-start.1 = (bf16[1,128,256]{1,2,0:T(8,128)(2,1)S(1)}, bf16[1,128,256]{1,2,0:T(8,128)(2,1)S(1)}, u32[]{:S(2)}, u32[]{:S(2)}) collective-permute-start(bf16[1,128,256]{1,2,0:T(8,128)(2,1)S(1)} %get-tuple-element.30), channel_id=1, source_target_pairs={{16,0},{32,16},{48,32},{64,48},{80,64},{96,80},{112,96},{17,1},{33... | collective-permute-start | bytes 196616 | tf_op jit(solution)/shard_map/ppermute | solution.py:25
  16.2 8.1 %copy-start.32 = (s32[16]{0:T(128)}, s32[16]{0:T(128)S(1)}, u32[]{:S(2)}) copy-start(s32[16]{0:T(128)S(1)} %multiply_add_fusion.1) | copy-start | bytes 196
  17.0 117.4 %all-to-all-start = ((bf16[16,1,2]{2,1,0:T(2,128)(2,1)}), bf16[16,1,2]{2,1,0:T(2,128)(2,1)}, u32[]{:S(2)}, u32[]{:S(2)}) async-start(bf16[16,1,2]{2,1,0:T(2,128)(2,1)} %all_to_all.16), calls=%async_computation | async-start | bytes 16384 | tf_op jit(solution)/shard_map/all_to_all | solution.py:202
  25.0 27.9 %copy-start.26 = (bf16[1,128,256]{1,2,0:T(8,128)(2,1)}, bf16[1,128,256]{1,2,0:T(8,128)(2,1)S(1)}, u32[]{:S(2)}) copy-start(bf16[1,128,256]{1,2,0:T(8,128)(2,1)S(1)} %collective-permute-done) | copy-start | bytes 196612
  25.0 27.9 %copy-start.24 = (bf16[1,128,256]{1,2,0:T(8,128)(2,1)}, bf16[1,128,256]{1,2,0:T(8,128)(2,1)S(1)}, u32[]{:S(2)}) copy-start(bf16[1,128,256]{1,2,0:T(8,128)(2,1)S(1)} %collective-permute-done.1) | copy-start | bytes 196612
  32.7 18.3 %collective-permute-start.2 = (bf16[34,1,256]{2,0,1:T(8,128)(2,1)S(1)}, bf16[34,1,256]{2,0,1:T(8,128)(2,1)S(1)}, u32[]{:S(2)}, u32[]{:S(2)}) collective-permute-start(bf16[34,1,256]{2,0,1:T(8,128)(2,1)S(1)} %copy.57), channel_id=1, source_target_pairs={{0,1},{1,2},{2,3},{3,4},{4,5},{5,6},{6,7},{7,8},{8,9},{9,10},{10,1... | collective-permute-start | bytes 52232 | tf_op jit(solution)/shard_map/ppermute | solution.py:22
  36.2 12.9 %collective-permute-start.3 = (bf16[34,1,256]{2,0,1:T(8,128)(2,1)S(1)}, bf16[34,1,256]{2,0,1:T(8,128)(2,1)S(1)}, u32[]{:S(2)}, u32[]{:S(2)}) collective-permute-start(bf16[34,1,256]{2,0,1:T(8,128)(2,1)S(1)} %copy.62), channel_id=1, source_target_pairs={{1,0},{2,1},{3,2},{4,3},{5,4},{6,5},{7,6},{8,7},{9,8},{10,9},{11,1... | collective-permute-start | bytes 52232 | tf_op jit(solution)/shard_map/ppermute | solution.py:25
  60.0 3.6 copy-start.5
  132.3 10.2 %copy-start.23 = (f32[256,256]{1,0:T(8,128)S(1)}, f32[256,256]{1,0:T(8,128)}, u32[]{:S(2)}) copy-start(f32[256,256]{1,0:T(8,128)} %param.14) | copy-start | bytes 786436
  132.4 10.3 %copy-start.22 = (f32[256,256]{1,0:T(8,128)S(1)}, f32[256,256]{1,0:T(8,128)}, u32[]{:S(2)}) copy-start(f32[256,256]{1,0:T(8,128)} %param.15) | copy-start | bytes 786436
  132.4 10.4 %copy-start.21 = (f32[256,256]{1,0:T(8,128)S(1)}, f32[256,256]{1,0:T(8,128)}, u32[]{:S(2)}) copy-start(f32[256,256]{1,0:T(8,128)} %param.16) | copy-start | bytes 786436
  134.4 11.6 %all-to-all-start.1 = ((bf16[16,2,256]{2,1,0:T(2,128)(2,1)}), bf16[16,2,256]{2,1,0:T(2,128)(2,1)S(1)}, u32[]{:S(2)}, u32[]{:S(2)}) async-start(bf16[16,2,256]{2,1,0:T(2,128)(2,1)} %reshape.228), calls=%async_computation.1 | async-start | bytes 32768 | tf_op jit(solution)/shard_map/all_to_all | solution.py:201
  142.9 85.8 %copy-start.33 = (s32[16]{0:T(128)S(1)}, s32[16]{0:T(128)}, u32[]{:S(2)}) copy-start(s32[16]{0:T(128)} %copy-done.32) | copy-start | bytes 196
  146.6 82.5 %copy-start.20 = (bf16[4,256,256]{2,1,0:T(8,128)(2,1)S(1)}, bf16[4,256,256]{2,1,0:T(8,128)(2,1)}, u32[]{:S(2)}) copy-start(bf16[4,256,256]{2,1,0:T(8,128)(2,1)} %param.13) | copy-start | bytes 1572868
  218.9 9.8 %all-to-all-start.2 = ((bf16[16,2,256]{2,1,0:T(2,128)(2,1)}), bf16[16,2,256]{2,1,0:T(2,128)(2,1)S(1)}, u32[]{:S(2)}, u32[]{:S(2)}) async-start(bf16[16,2,256]{2,1,0:T(2,128)(2,1)} %reshape.234), calls=%async_computation.2 | async-start | bytes 32768 | tf_op jit(solution)/shard_map/all_to_all | solution.py:218
  222.9 203.1 %all-reduce.2.cloned.1.call-start = ((), (), s32[]{:S(2)}) async-start(), calls=%async_computation.3 | async-start | bytes 4718592 | tf_op jit(solution)/shard_map/psum | solution.py:242
  242.7 11.1 %copy-start.27 = (bf16[1,128,256]{1,2,0:T(8,128)(2,1)S(1)}, bf16[1,128,256]{1,2,0:T(8,128)(2,1)}, u32[]{:S(2)}) copy-start(bf16[1,128,256]{1,2,0:T(8,128)(2,1)} %copy-done.26) | copy-start | bytes 196612
  242.7 12.5 %slice-start = ((s8[4456448]{0:T(1024)(128)(4,1)}), s8[262144]{0:T(1024)(128)(4,1)S(1)}, s32[]{:S(2)}) async-start(s8[4456448]{0:T(1024)(128)(4,1)} %bitcast.258), calls=%async_computation.4 | async-start | bytes 524288
  247.1 6.7 %copy-start.4 = (bf16[32,128,256]{1,2,0:T(8,128)(2,1)S(1)}, bf16[32,128,256]{1,2,0:T(8,128)(2,1)}, u32[]{:S(2)}) copy-start(bf16[32,128,256]{1,2,0:T(8,128)(2,1)} %copy-done.3) | copy-start | bytes 6291460
  247.1 8.2 %slice-start.1 = ((s8[4456448]{0:T(1024)(128)(4,1)}), s8[4194304]{0:T(1024)(128)(4,1)S(1)}, s32[]{:S(2)}) async-start(s8[4456448]{0:T(1024)(128)(4,1)} %bitcast.258), calls=%async_computation.5 | async-start | bytes 8388608
  247.1 9.9 %slice-start.2 = ((s8[4456448]{0:T(1024)(128)(4,1)}), s8[4194304]{0:T(1024)(128)(4,1)S(1)}, s32[]{:S(2)}) async-start(s8[4456448]{0:T(1024)(128)(4,1)} %bitcast.260), calls=%async_computation.6 | async-start | bytes 8388608
  250.3 22.4 %collective-permute-start.4 = (bf16[1,128,256]{2,1,0:T(8,128)(2,1)S(1)}, bf16[1,128,256]{2,1,0:T(8,128)(2,1)S(1)}, u32[]{:S(2)}, u32[]{:S(2)}) collective-permute-start(bf16[1,128,256]{2,1,0:T(8,128)(2,1)S(1)} %get-tuple-element.25), channel_id=1, source_target_pairs={{0,16},{16,32},{32,48},{48,64},{64,80},{80,96},{96,112},{1,17},{17... | collective-permute-start | bytes 196616 | tf_op jit(solution)/shard_map/ppermute | solution.py:22
  252.4 4.6 %slice-start.3 = ((s8[4456448]{0:T(1024)(128)(4,1)}), s8[262144]{0:T(1024)(128)(4,1)S(1)}, s32[]{:S(2)}) async-start(s8[4456448]{0:T(1024)(128)(4,1)} %bitcast.260), calls=%async_computation.7 | async-start | bytes 524288
  252.4 20.3 %collective-permute-start.5 = (bf16[1,128,256]{2,1,0:T(8,128)(2,1)S(1)}, bf16[1,128,256]{2,1,0:T(8,128)(2,1)S(1)}, u32[]{:S(2)}, u32[]{:S(2)}) collective-permute-start(bf16[1,128,256]{2,1,0:T(8,128)(2,1)S(1)} %get-tuple-element.26), channel_id=1, source_target_pairs={{16,0},{32,16},{48,32},{64,48},{80,64},{96,80},{112,96},{17,1},{33... | collective-permute-start | bytes 196616 | tf_op jit(solution)/shard_map/ppermute | solution.py:25
  272.7 6.6 %collective-permute-start.6 = (bf16[34,1,256]{2,1,0:T(2,128)(2,1)S(1)}, bf16[34,1,256]{2,1,0:T(2,128)(2,1)S(1)}, u32[]{:S(2)}, u32[]{:S(2)}) collective-permute-start(bf16[34,1,256]{2,1,0:T(2,128)(2,1)S(1)} %get-tuple-element.17), channel_id=1, source_target_pairs={{1,0},{2,1},{3,2},{4,3},{5,4},{6,5},{7,6},{8,7},{9,8},{10,9},{11,1... | collective-permute-start | bytes 52232 | tf_op jit(solution)/shard_map/ppermute | solution.py:25
  275.3 4.0 collective-permute-start.7
  284.6 3.5 copy-start.16
  284.6 3.5 copy-start.29
  (18 other events, 33.8 us)
Sparse Core Ops, SparseCore 0:
  272.8 153.1 all-reduce.1
where the time goes:
time: 441 us; the launch traced here: 436 us
  waiting for transfers between devices  137 us (31%)
  local copies, waits for them, and re-layouts  113 us (26%)
  blocking collectives  68 us (15%)
  matrix products  39.9 us (9%)
  starting transfers between devices  37.4 us (8%)
  other arithmetic  26.1 us (6%)
  between operations  15.2 us (3%)
    psum x1, waiting for transfers between devices, per_device(): conv_grad = lax.psum(local_grads, ('gy', 'gx'))  129 us
    psum x1, blocking collectives, per_device(): embedding = lax.psum(partial_sum, ('gy', 'gx')) * norm_scale  68 us
    slice x10, local copies, waits for them, and re-layouts, forward_taps(): padded[row_off:row_off + pix_rows, col_off:col_off + pix_cols]  38.9 us
    slice x4, local copies, waits for them, and re-layouts, strided_forward(): window = field[row_off::2, col_off::2].reshape(-1, channels)  21.1 us
    unnamed x81, local copies, waits for them, and re-layouts  17.7 us
    dot_general x9, matrix products, weight_taps(): lax.dot_general(window, flat_up, (((0,), (0,)), ((), ())), preferred_elem...  15.7 us
    ppermute x4, starting transfers between devices, extended(): lax.ppermute(lax.slice_in_dim(block, block.shape[dim] - width, None, axis...  12.6 us
    reshape x2, local copies, waits for them, and re-layouts, strided_backward(): return stacked.reshape(2 * half_rows, 2 * half_cols, -1)  12.3 us
  transfers between devices with their start and end apart: 12, of which 3 were waited for; matrix products, arithmetic and copies ran while one was open for 30% of the time, Pallas kernels for 0%

commit v1 on v0

v1 whole, which is shorter than its diff:
```python
import math

import jax
import jax.numpy as jnp
from jax import lax
from jax.experimental import pallas as pl
from jax.experimental.pallas import tpu as pltpu
from jax.sharding import PartitionSpec as P

MESH = pl.DeviceIdType.MESH
F32, BF16 = jnp.float32, jnp.bfloat16
HEADS = 4
attention_bias = -1.0
loss_scale = 512.0

GY, GX = 8, 16
ROWS, COLS, CH = 32, 128, 256
PAD = ROWS + 2
TILES, SLOTS = 16, 32
CONV_ROWS = 4
AXIS_ORDER = (("x", "y", "z"), ("y", "z", "x"), ("z", "x", "y"))
BARRIER_SIGNALS = 32


def exact_dot(a, b, a_dim=1, b_dim=0):
    return lax.dot_general(
        a, b, (((a_dim,), (b_dim,)), ((), ())),
        precision=lax.Precision.HIGHEST, preferred_element_type=F32,
    )


def half_dot(a, b, a_dim=1, b_dim=0):
    return lax.dot_general(
        a.astype(BF16), b.astype(BF16), (((a_dim,), (b_dim,)), ((), ())),
        preferred_element_type=F32,
    )


def three_parts(value):
    high = value.astype(BF16)
    rest = value - high.astype(F32)
    middle = rest.astype(BF16)
    low = (rest - middle.astype(F32)).astype(BF16)
    return high, middle, low


def iota(shape, dim):
    return lax.broadcasted_iota(jnp.int32, shape, dim)


def kernel(
    feat, tissue, owner, w_conv, w_stride, w_query, w_key, w_value, cot,
    emb_out, grad_out, conv_out,
    field, cols3, trans, slope, grad3, taps, taps_t, stride_w, proj, mask,
    sums, spread, send_l, send_r, halo_l, halo_r, gsend_l, gsend_r, ghalo_l, ghalo_r,
    tok_send, tok_recv, ret_send, ret_recv, own_rows, stride_back,
    local_w, pair_w, half_w, hop1, mid_w, hop2, hop3, full_w, emb_buf, out_buf, conv_buf,
    load_sem, halo_ssem, halo_rsem, ghalo_ssem, ghalo_rsem, tok_ssem, tok_rsem,
    ret_ssem, ret_rsem, red_ssem, red_rsem, pair_ssem, pair_rsem, emb_ssem, emb_rsem,
    out_sem,
):
    g, h = lax.axis_index("gy"), lax.axis_index("gx")
    x_hi, y = g // 4, g % 4
    z, x_lo, core = h // 4, (h // 2) % 2, h % 2
    position = {"x": 2 * x_hi + x_lo, "y": y, "z": z}
    partner = (g, h + 1 - 2 * core)

    def on_axis(axis, pos):
        if axis == "x":
            return ((pos // 2) * 4 + y, z * 4 + (pos % 2) * 2 + core)
        if axis == "y":
            return (x_hi * 4 + pos, h)
        return (g, pos * 4 + x_lo * 2 + core)

    up, down = (g + GY - 1) % GY, (g + 1) % GY
    left, right = (h + GX - 1) % GX, (h + 1) % GX

    def remote(src, dst, ssem, rsem, device):
        return pltpu.make_async_remote_copy(
            src_ref=src, dst_ref=dst, send_sem=ssem, recv_sem=rsem,
            device_id=device, device_id_type=MESH,
        )

    barrier = pltpu.get_barrier_semaphore()
    peers = [
        (up, h), (down, h), (g, left), (g, right),
        (up, left), (up, right), (down, left), (down, right),
    ]
    peers += [(g, (h + j) % GX) for j in range(1, GX)]
    for axis in ("x", "y", "z"):
        peers += [on_axis(axis, (position[axis] + j) % 4) for j in range(1, 4)]
    for device in peers:
        pl.semaphore_signal(barrier, inc=1, device_id=device, device_id_type=MESH)

    loads = [
        pltpu.make_async_copy(feat, field.at[pl.ds(1, ROWS)], load_sem.at[0]),
        pltpu.make_async_copy(w_conv, taps, load_sem.at[1]),
        pltpu.make_async_copy(w_stride, stride_w, load_sem.at[2]),
        pltpu.make_async_copy(w_query, proj.at[:, pl.ds(0, CH)], load_sem.at[3]),
        pltpu.make_async_copy(w_key, proj.at[:, pl.ds(CH, CH)], load_sem.at[4]),
        pltpu.make_async_copy(w_value, proj.at[:, pl.ds(2 * CH, CH)], load_sem.at[5]),
    ]
    for copy in loads:
        copy.start()
    loads[0].wait()

    def edge_columns(row, carry):
        send_l[pl.ds(row, 1), :] = field[row + 1, 0:16, :].astype(F32)[0:1, :]
        send_r[pl.ds(row, 1), :] = field[row + 1, COLS - 16 : COLS, :].astype(F32)[15:16, :]
        return carry

    lax.fori_loop(0, ROWS, edge_columns, 0)
    pl.semaphore_wait(barrier, BARRIER_SIGNALS)

    def halo_copies(first_row, last_row, low_row, high_row, col_l, col_r, got_l, got_r, ss, rs):
        top, bottom = pl.ds(0, 8), pl.ds(ROWS - 8, 8)
        return [
            remote(first_row, high_row, ss.at[0], rs.at[0], (up, h)),
            remote(last_row, low_row, ss.at[1], rs.at[1], (down, h)),
            remote(col_l, got_r.at[pl.ds(8, ROWS)], ss.at[2], rs.at[2], (g, left)),
            remote(col_r, got_l.at[pl.ds(8, ROWS)], ss.at[3], rs.at[3], (g, right)),
            remote(col_r.at[bottom], got_l.at[pl.ds(0, 8)], ss.at[4], rs.at[4], (down, right)),
            remote(col_r.at[top], got_l.at[pl.ds(40, 8)], ss.at[5], rs.at[5], (up, right)),
            remote(col_l.at[bottom], got_r.at[pl.ds(0, 8)], ss.at[6], rs.at[6], (down, left)),
            remote(col_l.at[top], got_r.at[pl.ds(40, 8)], ss.at[7], rs.at[7], (up, left)),
        ]

    halos = halo_copies(
        field.at[1], field.at[ROWS], field.at[0], field.at[PAD - 1],
        send_l, send_r, halo_l, halo_r, halo_ssem, halo_rsem,
    )
    for copy in halos:
        copy.start()

    has_left, has_right = h > 0, h < GX - 1
    has_up, has_down = g > 0, g < GY - 1

    def columns_of(center, before, after):
        spot = iota(center.shape, 0)
        low = jnp.where(spot == 0, before, pltpu.roll(center, 1, 0))
        high = jnp.where(spot == COLS - 1, after, pltpu.roll(center, COLS - 1, 0))
        return low, high

    def shift_row(row, carry):
        center = field[row]
        wide = center.astype(F32)
        cols3[row, :, 0:CH] = pltpu.roll(wide, 1, 0).astype(BF16)
        cols3[row, :, CH : 2 * CH] = center
        cols3[row, :, 2 * CH : 3 * CH] = pltpu.roll(wide, COLS - 1, 0).astype(BF16)
        return carry

    lax.fori_loop(1, ROWS + 1, shift_row, 0)
    for tile in range(TILES):
        tr, tc = tile // 8, tile % 8
        flag = tissue[tr, tc].astype(F32)
        mask[tr, tc * 16 : tc * 16 + 16, :] = jnp.zeros((16, CH), F32) + flag
        own_rows[tile : tile + 1, :] = jnp.zeros((1, 128), F32) + owner[0, 0, tile, 0].astype(F32)
    sums[...] = jnp.zeros_like(sums)
    loads[1].wait()

    for copy in halos:
        copy.wait_recv()

    def patch_row(row, carry):
        near = halo_l[pl.ds(7 + row, 1), :]
        far = halo_r[pl.ds(7 + row, 1), :]
        near = jnp.where(has_left, near, 0.0)
        far = jnp.where(has_right, far, 0.0)
        head = cols3[row, 0:16, 0:CH].astype(F32)
        tail = cols3[row, COLS - 16 : COLS, 2 * CH : 3 * CH].astype(F32)
        spot = iota(head.shape, 0)
        cols3[row, 0:16, 0:CH] = jnp.where(spot == 0, near, head).astype(BF16)
        cols3[row, COLS - 16 : COLS, 2 * CH : 3 * CH] = jnp.where(spot == 15, far, tail).astype(BF16)
        return carry

    lax.fori_loop(1, ROWS + 1, patch_row, 0)
    for row, present in ((0, has_up), (PAD - 1, has_down)):
        wide = jnp.where(present, field[row].astype(F32), 0.0)
        near = jnp.where(has_left & present, halo_l[7 + row : 8 + row, :], 0.0)
        far = jnp.where(has_right & present, halo_r[7 + row : 8 + row, :], 0.0)
        low, high = columns_of(wide, near, far)
        cols3[row, :, 0:CH] = low.astype(BF16)
        cols3[row, :, CH : 2 * CH] = wide.astype(BF16)
        cols3[row, :, 2 * CH : 3 * CH] = high.astype(BF16)

    def conv_block(source, weights, first, flipped):
        total = None
        for a in range(3):
            start = first + (2 - a if flipped else a)
            block = source[pl.ds(start, CONV_ROWS)].reshape(CONV_ROWS * COLS, 3 * CH)
            part = jnp.dot(block, weights[a], preferred_element_type=F32)
            total = part if total is None else total + part
        return total.reshape(CONV_ROWS, COLS, CH)

    def forward_block(step, carry):
        first = step * CONV_ROWS
        tr = step // (16 // CONV_ROWS)
        pre = conv_block(cols3, taps, first, False)
        gate = jax.nn.sigmoid(pre)
        slope[pl.ds(first, CONV_ROWS)] = gate * (1.0 + pre * (1.0 - gate))
        own = cols3[pl.ds(first + 1, CONV_ROWS), :, CH : 2 * CH].astype(F32)
        summed = (own + pre * gate * mask[tr][None]).astype(BF16).astype(F32)
        for a in range(2):
            total = sums[tr, a]
            for k in range(a, CONV_ROWS, 2):
                total = total + summed[k]
            sums[tr, a] = total
        return carry

    lax.fori_loop(0, ROWS // CONV_ROWS, forward_block, 0)

    lane_col, row_id = iota((16, COLS), 1), iota((16, COLS), 0)
    select = ((lane_col // 16 == row_id % 8) & (lane_col % 2 == row_id // 8)).astype(BF16)
    gathered = jnp.concatenate([sums[tr, a] for tr in range(2) for a in range(2)], axis=1)
    parts = three_parts(gathered)
    cell_sums = sum(jnp.dot(select, part, preferred_element_type=F32) for part in parts)
    loads[2].wait()
    pooled = jnp.zeros((TILES, CH), F32)
    for a in range(2):
        for b in range(2):
            tap = 2 * a + b
            lhs = jnp.concatenate(
                [cell_sums[b * 8 : b * 8 + 8, (2 * tr + a) * CH : (2 * tr + a + 1) * CH] for tr in range(2)],
                axis=0,
            )
            rhs = stride_w[tap * CH : (tap + 1) * CH, :]
            pooled = pooled + sum(
                jnp.dot(part, rhs, preferred_element_type=F32) for part in three_parts(lhs)
            )
    pooled = pooled * (1.0 / 64.0)
    inverse = lax.rsqrt(jnp.mean(pooled * pooled, axis=-1, keepdims=True) + 1e-05)
    normed = (pooled * inverse).astype(BF16)

    own = own_rows[...]
    lane0 = (iota((TILES, 128), 1) == 0).astype(F32)
    own_across = half_dot(lane0, own, 1, 1)
    same = (own[:, 0:TILES] == own_across) & (iota((TILES, TILES), 1) < iota((TILES, TILES), 0))
    rank = jnp.sum(same.astype(F32), axis=1, keepdims=True)
    slot = own * 8.0 + rank
    slot_lane = iota((TILES, 128), 1).astype(F32)
    place = (slot == slot_lane).astype(F32)
    place_flag = (slot + 2.0 == slot_lane).astype(F32)
    flag_rows = jnp.concatenate(
        [mask[tr, tc * 16 : tc * 16 + 1, :] for tr in range(2) for tc in range(8)], axis=0
    )
    table = half_dot(place, normed, 0, 0) + half_dot(place_flag, flag_rows, 0, 0)
    tok_send[...] = table.reshape(GX, 8, CH)
    tok_copies = [
        remote(
            tok_send.at[(h + j) % GX], tok_recv.at[h], tok_ssem.at[j], tok_rsem.at[j],
            (g, (h + j) % GX),
        )
        for j in range(1, GX)
    ]
    for copy in tok_copies:
        copy.start()
    tok_recv[h] = tok_send[h]

    def transpose_row(row, carry):
        lanes = pl.ds(pl.multiple_of(row * COLS, COLS), COLS)
        for b in range(3):
            trans[b, :, lanes] = cols3[row, :, b * CH : (b + 1) * CH].T
        return carry

    lax.fori_loop(0, PAD, transpose_row, 0)
    for k in range(3, 6):
        loads[k].wait()
    for copy in tok_copies:
        copy.wait_recv()

    got = tok_recv[...].reshape(GX * 8, CH)
    pick_row, pick_lane = iota((2 * SLOTS, GX * 8), 0), iota((2 * SLOTS, GX * 8), 1)
    index = pick_row % SLOTS
    pick = (pick_lane == (index // 2) * 8 + index % 2 + 2 * (pick_row // SLOTS)).astype(BF16)
    packed = half_dot(pick, got)
    tokens, flags = packed[0:SLOTS, :], packed[SLOTS : 2 * SLOTS, :]
    qkv = exact_dot(tokens, proj[...])
    query, key, value = qkv[:, 0:CH], qkv[:, CH : 2 * CH], qkv[:, 2 * CH : 3 * CH]
    head_of = iota((1, CH), 1) // (CH // HEADS)
    heads = [(head_of == k).astype(F32) for k in range(HEADS)]
    seed = cot[...] * (loss_scale / math.sqrt(GY * GX * TILES))
    query_by_head = jnp.concatenate([query * m for m in heads], axis=0)
    flag_by_head = jnp.concatenate([flags * m for m in heads], axis=0)
    scale = 1.0 / math.sqrt(CH // HEADS)
    scores = exact_dot(query_by_head, key, 1, 1) * scale
    first_lane = (iota((HEADS * SLOTS, CH), 1) == 0).astype(F32)
    key_flags = half_dot(first_lane, flags, 1, 1)
    gates = jax.nn.sigmoid(scores + attention_bias)
    column_sums = exact_dot(gates * key_flags, flag_by_head, 0, 0)
    d_value = column_sums * seed
    partial = jnp.sum(column_sums * value, axis=0, keepdims=True)
    d_weights = exact_dot(flag_by_head * seed, value, 1, 1)
    d_scores = d_weights * key_flags * gates * (1.0 - gates) * scale
    d_query_all = exact_dot(d_scores, key)
    d_query = sum(d_query_all[k * SLOTS : (k + 1) * SLOTS, :] * heads[k] for k in range(HEADS))
    d_key = exact_dot(d_scores, query_by_head, 0, 0)
    d_qkv = jnp.concatenate([d_query, d_key, d_value], axis=1)
    d_tokens = exact_dot(d_qkv, proj[...], 1, 1)
    back_row, back_lane = iota((GX * 8, SLOTS), 0), iota((GX * 8, SLOTS), 1)
    unpick = (back_row == (back_lane // 2) * 8 + back_lane % 2).astype(BF16)
    ret_send[...] = half_dot(unpick, d_tokens).reshape(GX, 8, CH)
    ret_copies = [
        remote(
            ret_send.at[(h + j) % GX], ret_recv.at[h], ret_ssem.at[j], ret_rsem.at[j],
            (g, (h + j) % GX),
        )
        for j in range(1, GX)
    ]
    for copy in ret_copies:
        copy.start()
    ret_recv[h] = ret_send[h]

    emb_steps = [("core", 2, core)] + [(axis, 4, position[axis]) for axis in ("x", "y", "z")]

    def emb_copies(step):
        axis, count, pos = emb_steps[step]
        copies = []
        for j in range(1, count):
            device = partner if axis == "core" else on_axis(axis, (pos + j) % 4)
            spot = emb_buf.at[step, pos]
            copies.append(
                remote(spot, spot, emb_ssem.at[step, j], emb_rsem.at[step, j], device)
            )
        return copies

    def emb_start(step, term):
        emb_buf[step, emb_steps[step][2]] = term
        for copy in emb_copies(step):
            copy.start()

    def emb_finish(step):
        for copy in emb_copies(step):
            copy.wait_recv()
        total = emb_buf[step, 0]
        for k in range(1, emb_steps[step][1]):
            total = total + emb_buf[step, k]
        return total

    emb_start(0, jnp.broadcast_to(partial, (8, CH)))

    for a in range(3):
        for b in range(3):
            taps_t[a, b * CH : (b + 1) * CH, :] = taps[a, b * CH : (b + 1) * CH, :].T

    for copy in ret_copies:
        copy.wait_recv()
    token_grad = half_dot(place, ret_recv[...].reshape(GX * 8, CH)) * flag_rows
    inner = jnp.mean(token_grad * pooled, axis=-1, keepdims=True)
    pooled_grad = token_grad * inverse - pooled * (inverse * inverse * inverse * inner)
    cell_grad = (pooled_grad * (1.0 / 64.0)).astype(BF16)
    stride_back[...] = half_dot(cell_grad, stride_w[...], 1, 1)
    odd = (iota((16, CH), 0) % 2) == 1
    for tile in range(TILES):
        tr, tc = tile // 8, tile % 8
        for a in range(2):
            even_row = stride_back[tile : tile + 1, (2 * a) * CH : (2 * a + 1) * CH]
            odd_row = stride_back[tile : tile + 1, (2 * a + 1) * CH : (2 * a + 2) * CH]
            spread[tr, a, tc * 16 : tc * 16 + 16, :] = jnp.where(odd, odd_row, even_row)

    def pre_grad_row(row, carry):
        tr = row // 16
        value = (spread[tr, row % 2] * mask[tr] * slope[row]).astype(BF16)
        grad3[row + 1, :, CH : 2 * CH] = value
        wide = value.astype(F32)
        gsend_l[pl.ds(row, 1), :] = wide[0:1, :]
        gsend_r[pl.ds(row, 1), :] = wide[COLS - 1 : COLS, :]
        return carry

    lax.fori_loop(0, ROWS, pre_grad_row, 0)
    middle = pl.ds(CH, CH)
    ghalos = halo_copies(
        grad3.at[1, :, middle], grad3.at[ROWS, :, middle],
        grad3.at[0, :, middle], grad3.at[PAD - 1, :, middle],
        gsend_l, gsend_r, ghalo_l, ghalo_r, ghalo_ssem, ghalo_rsem,
    )
    for copy in ghalos:
        copy.start()

    def pair_copy(k):
        rows = pl.ds(k * 768, 768)
        return remote(
            local_w.at[1 - core, rows], pair_w.at[rows], pair_ssem.at[0, k], pair_rsem.at[0, k], partner
        )

    def axis_copies(k, step, axis, source, target):
        pos = position[axis]
        copies = []
        for j in range(1, 4):
            to = (pos + j) % 4
            copies.append(
                remote(
                    source(to), target(j), red_ssem.at[step, k, j], red_rsem.at[step, k, j],
                    on_axis(axis, to),
                )
            )
        return copies

    def aligned(value):
        return pl.multiple_of(value, 16)

    def home_rows(k, count):
        first, second, _ = AXIS_ORDER[k]
        start = k * 768 + position[first] * 192
        if count == 48:
            start = start + position[second] * 48
        return pl.ds(aligned(start), count)

    def hop_copies(k, step):
        first, second, third = AXIS_ORDER[k]
        if step == 1:
            return axis_copies(
                k, 0, first,
                lambda to: half_w.at[pl.ds(aligned(k * 768 + to * 192), 192)],
                lambda j: hop1.at[k, j - 1],
            )
        if step == 2:
            return axis_copies(
                k, 1, second,
                lambda to: mid_w.at[k, pl.ds(aligned(to * 48), 48)],
                lambda j: hop2.at[k, j - 1],
            )
        if step == 3:
            spot = hop3.at[k, position[third]]
            return axis_copies(k, 2, third, lambda to: spot, lambda j: spot)
        if step == 4:
            spot = full_w.at[core, home_rows(k, 48)]
            return axis_copies(k, 3, second, lambda to: spot, lambda j: spot)
        spot = full_w.at[core, home_rows(k, 192)]
        return axis_copies(k, 4, first, lambda to: spot, lambda j: spot)

    def last_copy(k):
        spot = full_w.at[core, pl.ds(k * 768, 768)]
        return remote(spot, spot, pair_ssem.at[1, k], pair_rsem.at[1, k], partner)

    def reduce_step(k, step):
        first, second, third = AXIS_ORDER[k]
        if step == 0:
            pair_copy(k).start()
            return
        if step == 1:
            pair_copy(k).wait_recv()
            rows = pl.ds(k * 768, 768)
            both = local_w[core, rows].astype(F32) + pair_w[rows].astype(F32)
            half_w[rows] = both.astype(BF16)
        elif step == 7:
            last_copy(k).wait_recv()
            rows = pl.ds(k * 768, 768)
            for c in range(2):
                conv_buf[rows, c * 128 : c * 128 + 128] = full_w[c, rows].astype(F32) * (1.0 / loss_scale)
            return
        else:
            for copy in hop_copies(k, step - 1):
                copy.wait_recv()
            if step == 2:
                total = half_w[pl.ds(aligned(k * 768 + position[first] * 192), 192)].astype(F32)
                for j in range(3):
                    total = total + hop1[k, j].astype(F32)
                mid_w[k] = total.astype(BF16)
            elif step == 3:
                total = mid_w[k, pl.ds(aligned(position[second] * 48), 48)].astype(F32)
                for j in range(3):
                    total = total + hop2[k, j].astype(F32)
                hop3[k, position[third]] = total.astype(BF16)
            elif step == 4:
                total = hop3[k, 0].astype(F32)
                for j in range(1, 4):
                    total = total + hop3[k, j].astype(F32)
                full_w[core, home_rows(k, 48)] = total.astype(BF16)
        if step == 6:
            last_copy(k).start()
        else:
            for copy in hop_copies(k, step):
                copy.start()

    for a in range(3):
        def tap_of(b, carry):
            lhs = trans[b, :, a * COLS : a * COLS + ROWS * COLS]
            rhs = grad3[pl.ds(1, ROWS), :, CH : 2 * CH].reshape(ROWS * COLS, CH)
            part = jnp.dot(lhs, rhs, preferred_element_type=F32)
            rows = pl.ds(pl.multiple_of(a * 768 + b * CH, CH), CH)
            for c in range(2):
                local_w[c, rows, :] = part[:, c * 128 : c * 128 + 128].astype(BF16)
            return carry

        lax.fori_loop(0, 3, tap_of, 0)
        for k in range(a, -1, -1):
            reduce_step(k, a - k)
        if a:
            emb_start(a, emb_finish(a - 1))

    for copy in ghalos:
        copy.wait_recv()

    def grad_shift(row, carry):
        wide = grad3[row, :, CH : 2 * CH].astype(F32)
        near = jnp.where(has_left, ghalo_l[pl.ds(7 + row, 1), :], 0.0)
        far = jnp.where(has_right, ghalo_r[pl.ds(7 + row, 1), :], 0.0)
        low, high = columns_of(wide, near, far)
        grad3[row, :, 0:CH] = high.astype(BF16)
        grad3[row, :, 2 * CH : 3 * CH] = low.astype(BF16)
        return carry

    lax.fori_loop(0, PAD, grad_shift, 0)
    for row, present in ((0, has_up), (PAD - 1, has_down)):
        edge = grad3[row].astype(F32)
        grad3[row] = jnp.where(present, edge, 0.0).astype(BF16)

    def out_copy(first):
        rows = pl.ds(first, CONV_ROWS)
        return pltpu.make_async_copy(out_buf.at[rows], grad_out.at[rows], out_sem.at[0])

    def back_block(step, carry):
        first = step * CONV_ROWS
        tr = step // (16 // CONV_ROWS)
        total = conv_block(grad3, taps_t, first, True)
        for k in range(CONV_ROWS):
            out_buf[first + k] = (total[k] + spread[tr, k % 2]).astype(BF16)
        return carry

    blocks = ROWS // CONV_ROWS
    order = [
        [(2, 1), (1, 2), (0, 3)],
        [(0, 4)],
        [(2, 2), (1, 3)],
        [(0, 5)],
        [(2, 3), (1, 4)],
        [(0, 6)],
        [(2, 4), (1, 5)],
        [(0, 7)],
    ]
    for step in range(4):
        for k, phase in order[step]:
            reduce_step(k, phase)
        lax.fori_loop(2 * step, 2 * step + 2, back_block, 0)
    emb_start(3, emb_finish(2))
    whole_out = pltpu.make_async_copy(out_buf, grad_out, out_sem.at[0])
    whole_out.start()
    for step in range(4, 8):
        for k, phase in order[step]:
            reduce_step(k, phase)
    for k, phase in [(2, 5), (1, 6), (2, 6), (1, 7), (2, 7)]:
        reduce_step(k, phase)
    emb_out[...] = emb_finish(3)[0:1, :] * (1.0 / math.sqrt(GY * GX * TILES))
    conv_copy = pltpu.make_async_copy(conv_buf, conv_out, out_sem.at[1])
    conv_copy.start()

    for copy in halos + ghalos + tok_copies + ret_copies:
        copy.wait_send()
    for k in range(3):
        pair_copy(k).wait_send()
        for step in range(1, 6):
            for copy in hop_copies(k, step):
                copy.wait_send()
        last_copy(k).wait_send()
    for step in range(4):
        for copy in emb_copies(step):
            copy.wait_send()
    whole_out.wait()
    conv_copy.wait()


def per_device(features, tissue, owner_map, w_conv, w_stride, w_query, w_key, w_value, cotangent):
    whole = pl.BlockSpec(memory_space=pl.ANY)
    scalars = pl.BlockSpec(memory_space=pltpu.SMEM)
    vector = pl.BlockSpec(memory_space=pltpu.VMEM)
    dma = pltpu.SemaphoreType.DMA
    columns = pltpu.VMEM((ROWS, CH), F32)
    column_halo = pltpu.VMEM((ROWS + 16, CH), F32)
    slot_table = pltpu.VMEM((GX, 8, CH), F32)
    embedding, input_grad, conv_grad = pl.pallas_call(
        kernel,
        out_shape=(
            jax.ShapeDtypeStruct((1, CH), F32),
            jax.ShapeDtypeStruct((ROWS, COLS, CH), BF16),
            jax.ShapeDtypeStruct((9 * CH, CH), F32),
        ),
        in_specs=[whole, scalars, scalars, whole, whole, whole, whole, whole, vector],
        out_specs=(vector, whole, whole),
        scratch_shapes=[
            pltpu.VMEM((PAD, COLS, CH), BF16),
            pltpu.VMEM((PAD, COLS, 3 * CH), BF16),
            pltpu.VMEM((3, CH, PAD * COLS), BF16),
            pltpu.VMEM((ROWS, COLS, CH), F32),
            pltpu.VMEM((PAD, COLS, 3 * CH), BF16),
            pltpu.VMEM((3, 3 * CH, CH), BF16),
            pltpu.VMEM((3, 3 * CH, CH), BF16),
            pltpu.VMEM((4 * CH, CH), BF16),
            pltpu.VMEM((CH, 3 * CH), F32),
            pltpu.VMEM((2, COLS, CH), F32),
            pltpu.VMEM((2, 2, COLS, CH), F32),
            pltpu.VMEM((2, 2, COLS, CH), F32),
            columns, columns, column_halo, column_halo,
            columns, columns, column_halo, column_halo,
            slot_table, slot_table, slot_table, slot_table,
            pltpu.VMEM((TILES, 128), F32),
            pltpu.VMEM((TILES, 4 * CH), F32),
            pltpu.VMEM((2, 9 * CH, 128), BF16),
            pltpu.VMEM((9 * CH, 128), BF16),
            pltpu.VMEM((9 * CH, 128), BF16),
            pltpu.VMEM((3, 3, 192, 128), BF16),
            pltpu.VMEM((3, 192, 128), BF16),
            pltpu.VMEM((3, 3, 48, 128), BF16),
            pltpu.VMEM((3, 4, 48, 128), BF16),
            pltpu.VMEM((2, 9 * CH, 128), BF16),
            pltpu.VMEM((4, 4, 8, CH), F32),
            pltpu.VMEM((ROWS, COLS, CH), BF16),
            pltpu.VMEM((9 * CH, CH), F32),
            dma((6,)), dma((8,)), dma((8,)), dma((8,)), dma((8,)),
            dma((GX,)), dma((GX,)), dma((GX,)), dma((GX,)),
            dma((5, 3, 4)), dma((5, 3, 4)), dma((2, 3)), dma((2, 3)),
            dma((4, 4)), dma((4, 4)), dma((2,)),
        ],
        compiler_params=pltpu.CompilerParams(
            collective_id=0, has_side_effects=True, vmem_limit_bytes=60 * 1024 * 1024
        ),
    )(
        features, tissue, owner_map, w_conv.reshape(3, 3 * CH, CH),
        w_stride.reshape(4 * CH, CH), w_query, w_key, w_value, cotangent.reshape(1, CH),
    )
    return embedding.reshape(CH), input_grad, conv_grad.reshape(9, CH, CH)


def solution(mesh):
    in_specs = (
        P("gy", "gx", None), P("gy", "gx"), P("gy", "gx", None, None),
        P(), P(), P(), P(), P(), P(),
    )
    out_specs = (P(), P("gy", "gx", None), P())
    return jax.shard_map(
        per_device, mesh=mesh, in_specs=in_specs, out_specs=out_specs, check_vma=False
    )
```

time: 441 us -> 83.7 us (0.19); the launches traced: 436 us -> 83.5 us
  waiting for transfers between devices: 137 us -> 0 us
  local copies, waits for them, and re-layouts: 113 us -> 7.22 us
  Pallas kernels: 0 us -> 75.6 us
  blocking collectives: 68 us -> 0 us
  matrix products: 39.9 us -> 0 us
  starting transfers between devices: 37.4 us -> 0 us
  other arithmetic: 26.1 us -> 0 us
  between operations: 15.2 us -> 0.64 us
    psum x1 -> x0, waiting for transfers between devices: 129 us -> none  [per_device(): conv_grad = lax.psum(local_grads, ('gy', 'gx'))]
    pallas_call x0 -> x1, Pallas kernels: none -> 75.6 us  [per_device(): pl.pallas_call(kernel, out_shape=(jax.ShapeDtypeStruct((1, CH), F32), jax...]
    slice x21 -> x0, local copies, waits for them, and re-layouts: 69.5 us -> none  [the longest x10 38.9 us: forward_taps(): padded[row_off:row_off + pix_rows, col_off:col_off + pix_cols]]
    psum x1 -> x0, blocking collectives: 68 us -> none  [per_device(): embedding = lax.psum(partial_sum, ('gy', 'gx')) * norm_scale]
    dot_general x51 -> x0, matrix products: 39.9 us -> none  [the longest x9 15.7 us: weight_taps(): lax.dot_general(window, flat_up, (((0,), (0,)), ((), ())), preferred_elem...]
    ppermute x8 -> x0, starting transfers between devices: 20.4 us -> none  [the longest x4 12.6 us: extended(): lax.ppermute(lax.slice_in_dim(block, block.shape[dim] - width, None, axis...]
    all_to_all x3 -> x0, starting transfers between devices: 17 us -> none  [the longest x1 7.21 us: per_device(): lax.all_to_all(sent_flags, 'gx', split_axis=0, concat_axis=0, tiled=True)]
    reshape x12 -> x0, local copies, waits for them, and re-layouts: 14.2 us -> none  [the longest x2 12.3 us: strided_backward(): return stacked.reshape(2 * half_rows, 2 * half_cols, -1)]
  transfers between devices with their start and end apart: 12 -> 0, of which waited for: 3 -> 0; matrix products, arithmetic and copies ran while one was open for 30% -> 0% of each run, Pallas kernels for 0% -> 0%
where the time goes in v1:
time: 83.7 us; the launch traced here: 83.5 us
  Pallas kernels  75.6 us (90%)
  local copies, waits for them, and re-layouts  7.22 us (9%)
    pallas_call x1, Pallas kernels, per_device(): pl.pallas_call(kernel, out_shape=(jax.ShapeDtypeStruct((1, CH), F32), jax...  75.6 us
    unnamed x6, local copies, waits for them, and re-layouts  7.22 us

profile of v1, /device:TPU:1, one launch (start us, length us, event | category | flops | bytes accessed | tf_op | source)
XLA Modules:
  0.0 83.5 jit_solution(10850033068069472295)
XLA Ops:
  0.6 1.3 %copy.12.owner = s32[1,1,16,1]{3,2,1,0:T(8,128)} copy(s32[1,1,16,1]{2,3,1,0:T(1,128)} %param.11) | data formatting | bytes 128 | tf_op args[2]
  2.0 75.6 %shard_map.112 = (f32[1,256]{1,0:T(1,128)}, bf16[32,128,256]{2,1,0:T(8,128)(2,1)}, f32[2304,256]{1,0:T(8,128)}) custom-call(bf16[32,128,256]{2,1,0:T(8,128)(2,1)} %feat.1, s32[2,8]{1,0:T(2,128)} %tissue.1, s32[1,1,16,1]{3,2,1,0:T(8,128)} %copy.12.owner, bf16[3,768,256]{2,1,0:T(8,128)(2,1)} %bitcast.6, bf16[1024,256]{1,0:T(8,128)(2,1)} %bitcast.7, ...), custom_call_target="tpu_custom_call" | custom-call | tf_op jit(solution)/shard_map/pallas_call | solution.py:570
  77.6 1.2 %copy.16 = f32[256]{0:T(256)} copy(f32[256]{0:T(256)} %bitcast.8) | data formatting | bytes 2048
  78.8 0.0 copy-start
  78.8 3.3 %copy.17 = bf16[32,128,256]{2,1,0:T(8,128)(2,1)} copy(bf16[32,128,256]{2,1,0:T(8,128)(2,1)} %get-tuple-element.13) | data formatting | bytes 4194304
  82.1 0.0 copy-done
  82.1 1.4 %copy.18 = f32[9,256,256]{2,1,0:T(8,128)} copy(f32[9,256,256]{2,1,0:T(8,128)S(1)} %bitcast.5) | data formatting | bytes 4718592
Async XLA Ops:
  78.8 3.3 %copy-start = (f32[2304,256]{1,0:T(8,128)S(1)}, f32[2304,256]{1,0:T(8,128)}, u32[]{:S(2)}) copy-start(f32[2304,256]{1,0:T(8,128)} %get-tuple-element.8) | copy-start | bytes 7077892

commit v2 on v1

v2 whole, which is shorter than its diff:
```python
import math

import jax
import jax.numpy as jnp
from jax import lax
from jax.experimental import pallas as pl
from jax.experimental.pallas import tpu as pltpu
from jax.sharding import PartitionSpec as P

MESH = pl.DeviceIdType.MESH
F32, BF16 = jnp.float32, jnp.bfloat16
HEADS = 4
attention_bias = -1.0
loss_scale = 512.0

GY, GX = 8, 16
ROWS, COLS, CH = 32, 128, 256
PAD = ROWS + 2
TILES = 16
CONV_ROWS = 4
CHUNKS = ((0, 3, "xyz"), (3, 3, "yzx"), (6, 2, "zxy"), (8, 1, "xyz"))
BARRIER_SIGNALS = 23 + 15 * 3


def exact_dot(a, b, a_dim=1, b_dim=0):
    return lax.dot_general(
        a, b, (((a_dim,), (b_dim,)), ((), ())),
        precision=lax.Precision.HIGHEST, preferred_element_type=F32,
    )


def half_dot(a, b, a_dim=1, b_dim=0):
    return lax.dot_general(
        a.astype(BF16), b.astype(BF16), (((a_dim,), (b_dim,)), ((), ())),
        preferred_element_type=F32,
    )


def three_parts(value):
    high = value.astype(BF16)
    rest = value - high.astype(F32)
    middle = rest.astype(BF16)
    low = (rest - middle.astype(F32)).astype(BF16)
    return high, middle, low


def iota(shape, dim):
    return lax.broadcasted_iota(jnp.int32, shape, dim)


def kernel(
    feat, tissue, owner, w_conv, w_stride, w_query, w_key, w_value, cot,
    emb_out, out_buf, full_w,
    field, cols3, trans, slope, grad3, taps, taps_t, stride_w, proj, parts3, mask,
    sums, spread, send_l, send_r, halo_l, halo_r, gsend_l, gsend_r, ghalo_l, ghalo_r,
    edge_l, edge_r, tok_buf, code_rows, stride_back,
    local_w, pair_w, half_w, plane_w, line_w, emb_buf,
    load_sem, halo_ssem, halo_rsem, ghalo_ssem, ghalo_rsem, tok_ssem, tok_rsem,
    plane_ssem, plane_rsem, line_ssem, line_rsem, pair_ssem, pair_rsem, emb_ssem, emb_rsem,
):
    g, h = lax.axis_index("gy"), lax.axis_index("gx")
    x_hi, y = g // 4, g % 4
    z, x_lo, core = h // 4, (h // 2) % 2, h % 2
    position = {"x": 2 * x_hi + x_lo, "y": y, "z": z}
    partner = (g, h + 1 - 2 * core)

    def device_at(**moved):
        spot = dict(position, **moved)
        return (
            (spot["x"] // 2) * 4 + spot["y"],
            spot["z"] * 4 + (spot["x"] % 2) * 2 + core,
        )

    def on_axis(axis, pos):
        return device_at(**{axis: pos})

    def on_plane(axes, member):
        return device_at(**{axes[0]: member // 4, axes[1]: member % 4})

    def member_of(axes):
        return position[axes[0]] * 4 + position[axes[1]]

    up, down = (g + GY - 1) % GY, (g + 1) % GY
    left, right = (h + GX - 1) % GX, (h + 1) % GX

    def remote(src, dst, ssem, rsem, device):
        return pltpu.make_async_remote_copy(
            src_ref=src, dst_ref=dst, send_sem=ssem, recv_sem=rsem,
            device_id=device, device_id_type=MESH,
        )

    barrier = pltpu.get_barrier_semaphore()
    peers = [
        (up, h), (down, h), (g, left), (g, right),
        (up, left), (up, right), (down, left), (down, right),
    ]
    peers += [(g, (h + j) % GX) for j in range(1, GX)]
    for axes in ("xy", "yz", "zx"):
        peers += [on_plane(axes, (member_of(axes) + j) % 16) for j in range(1, 16)]
    for device in peers:
        pl.semaphore_signal(barrier, inc=1, device_id=device, device_id_type=MESH)

    loads = [
        pltpu.make_async_copy(feat, field.at[pl.ds(1, ROWS)], load_sem.at[0]),
        pltpu.make_async_copy(w_conv, taps, load_sem.at[1]),
        pltpu.make_async_copy(w_stride, stride_w, load_sem.at[2]),
        pltpu.make_async_copy(w_query, proj.at[:, pl.ds(0, CH)], load_sem.at[3]),
        pltpu.make_async_copy(w_key, proj.at[:, pl.ds(CH, CH)], load_sem.at[4]),
        pltpu.make_async_copy(w_value, proj.at[:, pl.ds(2 * CH, CH)], load_sem.at[5]),
    ]
    for copy in loads:
        copy.start()
    for tile in range(TILES):
        tr, tc = tile // 8, tile % 8
        flag = tissue[tr, tc].astype(F32)
        code = flag * (owner[0, tile].astype(F32) + 1.0)
        mask[tr, tc * 16 : tc * 16 + 16, :] = jnp.zeros((16, CH), F32) + flag
        code_rows[tile : tile + 1, :] = jnp.zeros((1, 128), F32) + code
    sums[...] = jnp.zeros_like(sums)
    loads[0].wait()

    def edge_columns(row, carry):
        send_l[pl.ds(row, 1), :] = field[row + 1, 0:16, :].astype(F32)[0:1, :]
        send_r[pl.ds(row, 1), :] = field[row + 1, COLS - 16 : COLS, :].astype(F32)[15:16, :]
        return carry

    lax.fori_loop(0, ROWS, edge_columns, 0)
    def halo_copies(first_row, last_row, low_row, high_row, col_l, col_r, got_l, got_r, ss, rs):
        top, bottom = pl.ds(0, 8), pl.ds(ROWS - 8, 8)
        return [
            remote(first_row, high_row, ss.at[0], rs.at[0], (up, h)),
            remote(last_row, low_row, ss.at[1], rs.at[1], (down, h)),
            remote(col_l, got_r.at[pl.ds(8, ROWS)], ss.at[2], rs.at[2], (g, left)),
            remote(col_r, got_l.at[pl.ds(8, ROWS)], ss.at[3], rs.at[3], (g, right)),
            remote(col_r.at[bottom], got_l.at[pl.ds(0, 8)], ss.at[4], rs.at[4], (down, right)),
            remote(col_r.at[top], got_l.at[pl.ds(40, 8)], ss.at[5], rs.at[5], (up, right)),
            remote(col_l.at[bottom], got_r.at[pl.ds(0, 8)], ss.at[6], rs.at[6], (down, left)),
            remote(col_l.at[top], got_r.at[pl.ds(40, 8)], ss.at[7], rs.at[7], (up, left)),
        ]

    has_left, has_right = h > 0, h < GX - 1
    has_up, has_down = g > 0, g < GY - 1

    def columns_of(center, before, after):
        spot = iota(center.shape, 0)
        low = jnp.where(spot == 0, before, pltpu.roll(center, 1, 0))
        high = jnp.where(spot == COLS - 1, after, pltpu.roll(center, COLS - 1, 0))
        return low, high

    def shift_row(row, carry):
        center = field[row]
        low, high = columns_of(center.astype(F32), 0.0, 0.0)
        cols3[row, :, 0:CH] = low.astype(BF16)
        cols3[row, :, CH : 2 * CH] = center
        cols3[row, :, 2 * CH : 3 * CH] = high.astype(BF16)
        return carry

    lax.fori_loop(1, ROWS + 1, shift_row, 0)
    loads[1].wait()

    def conv_block(source, weights, first, flipped):
        total = None
        for a in range(3):
            start = first + (2 - a if flipped else a)
            block = source[pl.ds(start, CONV_ROWS)].reshape(CONV_ROWS * COLS, 3 * CH)
            part = jnp.dot(block, weights[a], preferred_element_type=F32)
            total = part if total is None else total + part
        return total.reshape(CONV_ROWS, COLS, CH)

    def forward_block(step, carry):
        first = step * CONV_ROWS
        tr = step // (16 // CONV_ROWS)
        pre = conv_block(cols3, taps, first, False)
        for k in range(CONV_ROWS):
            edge_l[pl.ds(first + k, 1), :] = pre[k, 0:1, :]
            edge_r[pl.ds(first + k, 1), :] = pre[k, COLS - 1 : COLS, :]
        gate = jax.nn.sigmoid(pre)
        slope[pl.ds(first, CONV_ROWS)] = gate * (1.0 + pre * (1.0 - gate))
        own = cols3[pl.ds(first + 1, CONV_ROWS), :, CH : 2 * CH].astype(F32)
        summed = (own + pre * gate * mask[tr][None]).astype(BF16).astype(F32)
        for a in range(2):
            total = sums[tr, a]
            for k in range(a, CONV_ROWS, 2):
                total = total + summed[k]
            sums[tr, a] = total
        return carry

    lax.fori_loop(1, 3, forward_block, 0)
    pl.semaphore_wait(barrier, BARRIER_SIGNALS)
    halos = halo_copies(
        field.at[1], field.at[ROWS], field.at[0], field.at[PAD - 1],
        send_l, send_r, halo_l, halo_r, halo_ssem, halo_rsem,
    )
    for copy in halos:
        copy.start()
    lax.fori_loop(3, 7, forward_block, 0)

    def transpose_middle(row, carry):
        lanes = pl.ds(pl.multiple_of(row * COLS, COLS), COLS)
        trans[1, :, lanes] = cols3[row, :, CH : 2 * CH].T
        return carry

    lax.fori_loop(1, ROWS + 1, transpose_middle, 0)
    for a in range(3):
        for b in range(3):
            taps_t[a, b * CH : (b + 1) * CH, :] = taps[a, b * CH : (b + 1) * CH, :].T
    for k in range(3, 6):
        loads[k].wait()
    for k, part in enumerate(three_parts(proj[...])):
        parts3[k] = part
    for copy in halos:
        copy.wait_recv()

    def patch_row(row, carry):
        near = halo_l[pl.ds(7 + row, 1), :]
        far = halo_r[pl.ds(7 + row, 1), :]
        near = jnp.where(has_left, near, 0.0)
        far = jnp.where(has_right, far, 0.0)
        head = cols3[row, 0:16, 0:CH].astype(F32)
        tail = cols3[row, COLS - 16 : COLS, 2 * CH : 3 * CH].astype(F32)
        spot = iota(head.shape, 0)
        cols3[row, 0:16, 0:CH] = jnp.where(spot == 0, near, head).astype(BF16)
        cols3[row, COLS - 16 : COLS, 2 * CH : 3 * CH] = jnp.where(spot == 15, far, tail).astype(BF16)
        return carry

    lax.fori_loop(1, ROWS + 1, patch_row, 0)
    for row, present in ((0, has_up), (PAD - 1, has_down)):
        wide = jnp.where(present, field[row].astype(F32), 0.0)
        near = jnp.where(has_left & present, halo_l[7 + row : 8 + row, :], 0.0)
        far = jnp.where(has_right & present, halo_r[7 + row : 8 + row, :], 0.0)
        low, high = columns_of(wide, near, far)
        cols3[row, :, 0:CH] = low.astype(BF16)
        cols3[row, :, CH : 2 * CH] = wide.astype(BF16)
        cols3[row, :, 2 * CH : 3 * CH] = high.astype(BF16)

    lax.fori_loop(0, 2, lambda i, carry: forward_block(i * 7, carry), 0)
    row_of = iota((ROWS, CH), 0)
    inner_row = (row_of >= CONV_ROWS) & (row_of < ROWS - CONV_ROWS)

    def fix_edge(got, present, edge, own, tap_at, col):
        terms = [jnp.where(present, got[7 + a : 7 + a + ROWS, :], 0.0).astype(BF16) for a in range(3)]
        pre = edge[...]
        flag = jnp.where(row_of < 16, mask[0, col : col + 1, :], mask[1, col : col + 1, :])
        old = (own[...] + pre * jax.nn.sigmoid(pre) * flag).astype(BF16).astype(F32)
        for a in range(3):
            pre = pre + jnp.dot(
                terms[a], taps[a, tap_at * CH : (tap_at + 1) * CH, :], preferred_element_type=F32
            )
        gate = jax.nn.sigmoid(pre)
        new = (own[...] + pre * gate * flag).astype(BF16).astype(F32)
        slant = gate * (1.0 + pre * (1.0 - gate))
        change = jnp.where(inner_row, new - old, 0.0)
        for tr in range(2):
            for a in range(2):
                part = jnp.where((row_of // 16 == tr) & (row_of % 2 == a), change, 0.0)
                sums[tr, a, col : col + 1, :] = sums[tr, a, col : col + 1, :] + jnp.sum(
                    part, axis=0, keepdims=True
                )
        for row in range(CONV_ROWS, ROWS - CONV_ROWS):
            slope[row, col : col + 1, :] = slant[row : row + 1, :]

    fix_edge(halo_l, has_left, edge_l, send_l, 0, 0)
    fix_edge(halo_r, has_right, edge_r, send_r, 2, COLS - 1)


    lane_col, row_id = iota((16, COLS), 1), iota((16, COLS), 0)
    select = ((lane_col // 16 == row_id % 8) & (lane_col % 2 == row_id // 8)).astype(BF16)
    gathered = jnp.concatenate([sums[tr, a] for tr in range(2) for a in range(2)], axis=1)
    parts = three_parts(gathered)
    cell_sums = sum(jnp.dot(select, part, preferred_element_type=F32) for part in parts)
    loads[2].wait()
    pooled = jnp.zeros((TILES, CH), F32)
    for a in range(2):
        for b in range(2):
            tap = 2 * a + b
            lhs = jnp.concatenate(
                [cell_sums[b * 8 : b * 8 + 8, (2 * tr + a) * CH : (2 * tr + a + 1) * CH] for tr in range(2)],
                axis=0,
            )
            rhs = stride_w[tap * CH : (tap + 1) * CH, :]
            pooled = pooled + sum(
                jnp.dot(part, rhs, preferred_element_type=F32) for part in three_parts(lhs)
            )
    pooled = pooled * (1.0 / 64.0)
    inverse = lax.rsqrt(jnp.mean(pooled * pooled, axis=-1, keepdims=True) + 1e-05)
    normed = (pooled * inverse).astype(BF16)

    code = code_rows[...]
    tok_buf[h, :, 0:CH] = normed
    tok_buf[h, :, CH : CH + 128] = code.astype(BF16)
    tok_copies = [
        remote(tok_buf.at[h], tok_buf.at[h], tok_ssem.at[j], tok_rsem.at[j], (g, (h + j) % GX))
        for j in range(1, GX)
    ]
    for copy in tok_copies:
        copy.start()

    head_of = iota((1, CH), 1) // (CH // HEADS)
    heads = [(head_of == k).astype(F32) for k in range(HEADS)]

    def by_head(rows):
        return jnp.concatenate([rows * m for m in heads], axis=0)

    def join_heads(rows):
        return sum(rows[k * TILES : (k + 1) * TILES, :] * heads[k] for k in range(HEADS))

    own_qkv = sum(jnp.dot(normed, parts3[k], preferred_element_type=F32) for k in range(3))
    own_value = own_qkv[:, 2 * CH : 3 * CH]
    query_by_head, key_by_head = by_head(own_qkv[:, 0:CH]), by_head(own_qkv[:, CH : 2 * CH])
    seed = cot[...] * (loss_scale / math.sqrt(GY * GX * TILES))
    seed_by_head = by_head(jnp.broadcast_to(seed, (8, CH)))
    value_seed = exact_dot(seed_by_head, proj[:, 2 * CH : 3 * CH], 1, 1)
    own_value_seed = jnp.sum(by_head(own_value * seed), axis=1, keepdims=True)

    def transpose_row(row, carry):
        lanes = pl.ds(pl.multiple_of(row * COLS, COLS), COLS)
        for b in (0, 2):
            trans[b, :, lanes] = cols3[row, :, b * CH : (b + 1) * CH].T
        return carry

    lax.fori_loop(0, PAD, transpose_row, 0)
    for row in (0, PAD - 1):
        trans[1, :, row * COLS : (row + 1) * COLS] = cols3[row, :, CH : 2 * CH].T
    for copy in tok_copies:
        copy.wait_recv()

    everyone = tok_buf[:, :, 0:CH].reshape(GX * TILES, CH)
    codes = tok_buf[:, :, CH : CH + 128].reshape(GX * TILES, 128)
    all_qk = sum(
        jnp.dot(everyone, parts3[k, :, 0 : 2 * CH], preferred_element_type=F32) for k in range(3)
    )
    all_query, all_key = all_qk[:, 0:CH], all_qk[:, CH : 2 * CH]
    lane0 = (iota((TILES, 128), 1) == 0).astype(F32)
    codes_across = half_dot(lane0, codes, 1, 1)
    allowed = ((codes_across == code[:, 0:1]) & (codes_across > 0.5)).astype(F32)
    allowed = jnp.concatenate([allowed] * HEADS, axis=0)
    scale = 1.0 / math.sqrt(CH // HEADS)
    as_query = jax.nn.sigmoid(exact_dot(query_by_head, all_key, 1, 1) * scale + attention_bias)
    as_key = jax.nn.sigmoid(exact_dot(key_by_head, all_query, 1, 1) * scale + attention_bias)
    weight_sums = jnp.sum(as_key * allowed, axis=1, keepdims=True)
    head_sums = join_heads(jnp.broadcast_to(weight_sums, (HEADS * TILES, CH)))
    partial = jnp.sum(head_sums * own_value, axis=0, keepdims=True)
    d_value = head_sums * seed
    across = sum(half_dot(part, everyone, 1, 1) for part in three_parts(value_seed))
    across = jnp.concatenate([across[8 * k : 8 * k + 8, :] for k in range(HEADS) for _ in range(2)], axis=0)
    d_as_query = across * allowed * as_query * (1.0 - as_query) * scale
    d_as_key = own_value_seed * allowed * as_key * (1.0 - as_key) * scale
    d_query = join_heads(exact_dot(d_as_query, all_key))
    d_key = join_heads(exact_dot(d_as_key, all_query))
    d_qkv = three_parts(jnp.concatenate([d_query, d_key, d_value], axis=1))
    d_tokens = jnp.zeros((TILES, CH), F32)
    for k in range(3):
        lhs = jnp.concatenate(d_qkv[: 3 - k], axis=0)
        product = half_dot(lhs, parts3[k], 1, 1)
        for part in range(3 - k):
            d_tokens = d_tokens + product[part * TILES : (part + 1) * TILES, :]
    token_grad = d_tokens.astype(BF16).astype(F32)

    emb_steps = [("core", 2, core)] + [(axis, 4, position[axis]) for axis in ("x", "y", "z")]

    def emb_copies(step):
        axis, count, pos = emb_steps[step]
        copies = []
        for j in range(1, count):
            device = partner if axis == "core" else on_axis(axis, (pos + j) % 4)
            spot = emb_buf.at[step, pos]
            copies.append(
                remote(spot, spot, emb_ssem.at[step, j], emb_rsem.at[step, j], device)
            )
        return copies

    def emb_start(step, term):
        emb_buf[step, emb_steps[step][2]] = term
        for copy in emb_copies(step):
            copy.start()

    def emb_finish(step):
        for copy in emb_copies(step):
            copy.wait_recv()
        total = emb_buf[step, 0]
        for k in range(1, emb_steps[step][1]):
            total = total + emb_buf[step, k]
        return total

    emb_start(0, jnp.broadcast_to(partial, (8, CH)))

    inner = jnp.mean(token_grad * pooled, axis=-1, keepdims=True)
    pooled_grad = token_grad * inverse - pooled * (inverse * inverse * inverse * inner)
    cell_grad = (pooled_grad * (1.0 / 64.0)).astype(BF16)
    stride_back[...] = half_dot(cell_grad, stride_w[...], 1, 1)
    odd = (iota((16, CH), 0) % 2) == 1
    for tile in range(TILES):
        tr, tc = tile // 8, tile % 8
        for a in range(2):
            even_row = stride_back[tile : tile + 1, (2 * a) * CH : (2 * a + 1) * CH]
            odd_row = stride_back[tile : tile + 1, (2 * a + 1) * CH : (2 * a + 2) * CH]
            spread[tr, a, tc * 16 : tc * 16 + 16, :] = jnp.where(odd, odd_row, even_row)

    def pre_grad_row(row, carry):
        tr = row // 16
        value = (spread[tr, row % 2] * mask[tr] * slope[row]).astype(BF16)
        grad3[row + 1, :, CH : 2 * CH] = value
        wide = value.astype(F32)
        gsend_l[pl.ds(row, 1), :] = wide[0:1, :]
        gsend_r[pl.ds(row, 1), :] = wide[COLS - 1 : COLS, :]
        return carry

    lax.fori_loop(0, ROWS, pre_grad_row, 0)
    middle = pl.ds(CH, CH)
    ghalos = halo_copies(
        grad3.at[1, :, middle], grad3.at[ROWS, :, middle],
        grad3.at[0, :, middle], grad3.at[PAD - 1, :, middle],
        gsend_l, gsend_r, ghalo_l, ghalo_r, ghalo_ssem, ghalo_rsem,
    )
    for copy in ghalos:
        copy.start()

    def chunk_rows(k):
        first, count, _ = CHUNKS[k]
        return pl.ds(first * CH, count * CH)

    def shard_rows(k):
        first, count, _ = CHUNKS[k]
        return pl.ds(first * 16, count * 16)

    def block_rows(k, member):
        first, count, _ = CHUNKS[k]
        return pl.ds(pl.multiple_of(first * CH + member * (count * 16), 16), count * 16)

    def pair_copy(k):
        rows = chunk_rows(k)
        return remote(
            local_w.at[1 - core, rows], pair_w.at[rows], pair_ssem.at[0, k], pair_rsem.at[0, k], partner
        )

    def plane_copies(k, back):
        axes = CHUNKS[k][2]
        me = member_of(axes)
        copies = []
        for j in range(1, 16):
            to = (me + j) % 16
            if back:
                source = target = full_w.at[core, block_rows(k, me)]
            else:
                source, target = half_w.at[block_rows(k, to)], plane_w.at[j - 1, shard_rows(k)]
            copies.append(
                remote(
                    source, target, plane_ssem.at[back, k, j], plane_rsem.at[back, k, j],
                    on_plane(axes, to),
                )
            )
        return copies

    def line_copies(k):
        axis = CHUNKS[k][2][2]
        pos = position[axis]
        spot = line_w.at[pos, shard_rows(k)]
        return [
            remote(
                spot, spot, line_ssem.at[k, j], line_rsem.at[k, j], on_axis(axis, (pos + j) % 4)
            )
            for j in range(1, 4)
        ]

    def last_copy(k):
        spot = full_w.at[core, chunk_rows(k)]
        return remote(spot, spot, pair_ssem.at[1, k], pair_rsem.at[1, k], partner)

    def reduce_step(k, step):
        axes = CHUNKS[k][2]
        rows, shard = chunk_rows(k), shard_rows(k)
        if step == 0:
            pair_copy(k).start()
        elif step == 1:
            pair_copy(k).wait_recv()
            both = local_w[core, rows].astype(F32) + pair_w[rows].astype(F32)
            half_w[rows] = both.astype(BF16)
            for copy in plane_copies(k, 0):
                copy.start()
        elif step == 2:
            for copy in plane_copies(k, 0):
                copy.wait_recv()
            total = half_w[block_rows(k, member_of(axes))].astype(F32)
            for j in range(15):
                total = total + plane_w[j, shard].astype(F32)
            line_w[position[axes[2]], shard] = total.astype(BF16)
            for copy in line_copies(k):
                copy.start()
        elif step == 3:
            for copy in line_copies(k):
                copy.wait_recv()
            total = line_w[0, shard].astype(F32)
            for j in range(1, 4):
                total = total + line_w[j, shard].astype(F32)
            full_w[core, block_rows(k, member_of(axes))] = total.astype(BF16)
            for copy in plane_copies(k, 1):
                copy.start()
        elif step == 4:
            for copy in plane_copies(k, 1):
                copy.wait_recv()
            last_copy(k).start()
        else:
            last_copy(k).wait_recv()

    def tap_of(tap, carry):
        a, b = tap // 3, tap % 3
        lhs = trans[b, :, pl.ds(pl.multiple_of(a * COLS, COLS), ROWS * COLS)]
        rhs = grad3[pl.ds(1, ROWS), :, CH : 2 * CH].reshape(ROWS * COLS, CH)
        part = jnp.dot(lhs, rhs, preferred_element_type=F32)
        rows = pl.ds(pl.multiple_of(tap * CH, CH), CH)
        for c in range(2):
            local_w[c, rows, :] = part[:, c * 128 : c * 128 + 128].astype(BF16)
        return carry

    after_taps = [[(0, 0)], [(1, 0), (0, 1)], [(2, 0), (1, 1)], [(3, 0), (2, 1)]]
    for k, (first, count, _) in enumerate(CHUNKS):
        lax.fori_loop(first, first + count, tap_of, 0)
        for chunk, step in after_taps[k]:
            reduce_step(chunk, step)
        if k < 3:
            emb_start(k + 1, emb_finish(k))

    for copy in ghalos:
        copy.wait_recv()

    def grad_shift(row, carry):
        wide = grad3[row, :, CH : 2 * CH].astype(F32)
        near = jnp.where(has_left, ghalo_l[pl.ds(7 + row, 1), :], 0.0)
        far = jnp.where(has_right, ghalo_r[pl.ds(7 + row, 1), :], 0.0)
        low, high = columns_of(wide, near, far)
        grad3[row, :, 0:CH] = high.astype(BF16)
        grad3[row, :, 2 * CH : 3 * CH] = low.astype(BF16)
        return carry

    lax.fori_loop(0, PAD // 2, grad_shift, 0)
    reduce_step(3, 1)
    lax.fori_loop(PAD // 2, PAD, grad_shift, 0)
    for row, present in ((0, has_up), (PAD - 1, has_down)):
        edge = grad3[row].astype(F32)
        grad3[row] = jnp.where(present, edge, 0.0).astype(BF16)

    def back_block(step, carry):
        first = step * CONV_ROWS
        tr = step // (16 // CONV_ROWS)
        total = conv_block(grad3, taps_t, first, True)
        for k in range(CONV_ROWS):
            out_buf[first + k] = (total[k] + spread[tr, k % 2]).astype(BF16)
        return carry

    order = [[(0, 2)], [(1, 2)], [(2, 2), (0, 3)], [(3, 2), (1, 3)]]
    for part in range(4):
        for chunk, step in order[part]:
            reduce_step(chunk, step)
        lax.fori_loop(2 * part, 2 * part + 2, back_block, 0)
    emb_out[...] = emb_finish(3)[0:1, :] * (1.0 / math.sqrt(GY * GX * TILES))
    for step in (3, 4, 5):
        for chunk in range(4):
            if step > 3 or chunk > 1:
                reduce_step(chunk, step)

    for copy in halos + ghalos + tok_copies:
        copy.wait_send()
    for k in range(len(CHUNKS)):
        for copy in [pair_copy(k), last_copy(k)] + line_copies(k):
            copy.wait_send()
        for back in range(2):
            for copy in plane_copies(k, back):
                copy.wait_send()
    for step in range(4):
        for copy in emb_copies(step):
            copy.wait_send()


def finish(emb, grad, conv, emb_out, grad_out, conv_out, wide, sem):
    copies = [
        pltpu.make_async_copy(emb, emb_out, sem.at[0]),
        pltpu.make_async_copy(grad.at[pl.ds(0, 16)], grad_out.at[pl.ds(0, 16)], sem.at[1]),
        pltpu.make_async_copy(grad.at[pl.ds(16, 16)], grad_out.at[pl.ds(16, 16)], sem.at[2]),
    ]
    for copy in copies:
        copy.start()
    for k in range(3):
        rows = pl.ds(k * 3 * CH, 3 * CH)
        for c in range(2):
            wide[rows, c * 128 : c * 128 + 128] = conv[c, rows].astype(F32) * (1.0 / loss_scale)
        copy = pltpu.make_async_copy(wide.at[rows], conv_out.at[rows], sem.at[3 + k])
        copy.start()
        copies.append(copy)
    for copy in copies:
        copy.wait()


def per_device(features, tissue, owner_map, w_conv, w_stride, w_query, w_key, w_value, cotangent):
    whole = pl.BlockSpec(memory_space=pl.ANY)
    scalars = pl.BlockSpec(memory_space=pltpu.SMEM)
    vector = pl.BlockSpec(memory_space=pltpu.VMEM)
    dma = pltpu.SemaphoreType.DMA
    columns = pltpu.VMEM((ROWS, CH), F32)
    column_halo = pltpu.VMEM((ROWS + 16, CH), F32)
    embedding, input_grad, conv_grad = pl.pallas_call(
        kernel,
        out_shape=(
            pltpu.VMEM((1, CH), F32),
            pltpu.VMEM((ROWS, COLS, CH), BF16),
            pltpu.VMEM((2, 9 * CH, 128), BF16),
        ),
        in_specs=[whole, scalars, scalars, whole, whole, whole, whole, whole, vector],
        out_specs=(vector, vector, vector),
        scratch_shapes=[
            pltpu.VMEM((PAD, COLS, CH), BF16),
            pltpu.VMEM((PAD, COLS, 3 * CH), BF16),
            pltpu.VMEM((3, CH, PAD * COLS), BF16),
            pltpu.VMEM((ROWS, COLS, CH), F32),
            pltpu.VMEM((PAD, COLS, 3 * CH), BF16),
            pltpu.VMEM((3, 3 * CH, CH), BF16),
            pltpu.VMEM((3, 3 * CH, CH), BF16),
            pltpu.VMEM((4 * CH, CH), BF16),
            pltpu.VMEM((CH, 3 * CH), F32),
            pltpu.VMEM((3, CH, 3 * CH), BF16),
            pltpu.VMEM((2, COLS, CH), F32),
            pltpu.VMEM((2, 2, COLS, CH), F32),
            pltpu.VMEM((2, 2, COLS, CH), F32),
            columns, columns, column_halo, column_halo,
            columns, columns, column_halo, column_halo,
            columns, columns,
            pltpu.VMEM((GX, TILES, CH + 128), BF16),
            pltpu.VMEM((TILES, 128), F32),
            pltpu.VMEM((TILES, 4 * CH), F32),
            pltpu.VMEM((2, 9 * CH, 128), BF16),
            pltpu.VMEM((9 * CH, 128), BF16),
            pltpu.VMEM((9 * CH, 128), BF16),
            pltpu.VMEM((15, 144, 128), BF16),
            pltpu.VMEM((4, 144, 128), BF16),
            pltpu.VMEM((4, 4, 8, CH), F32),
            dma((6,)), dma((8,)), dma((8,)), dma((8,)), dma((8,)),
            dma((GX,)), dma((GX,)),
            dma((2, 4, 16)), dma((2, 4, 16)), dma((4, 4)), dma((4, 4)), dma((2, 4)), dma((2, 4)),
            dma((4, 4)), dma((4, 4)),
        ],
        compiler_params=pltpu.CompilerParams(
            collective_id=0, has_side_effects=True, vmem_limit_bytes=56 * 1024 * 1024
        ),
    )(
        features, tissue, owner_map.reshape(1, TILES), w_conv.reshape(3, 3 * CH, CH),
        w_stride.reshape(4 * CH, CH), w_query, w_key, w_value, cotangent.reshape(1, CH),
    )
    embedding, input_grad, conv_grad = pl.pallas_call(
        finish,
        out_shape=(
            jax.ShapeDtypeStruct((1, CH), F32),
            jax.ShapeDtypeStruct((ROWS, COLS, CH), BF16),
            jax.ShapeDtypeStruct((9 * CH, CH), F32),
        ),
        in_specs=[vector, vector, vector],
        out_specs=(whole, whole, whole),
        scratch_shapes=[pltpu.VMEM((9 * CH, CH), F32), dma((6,))],
    )(embedding, input_grad, conv_grad)
    return embedding.reshape(CH), input_grad, conv_grad.reshape(9, CH, CH)


def solution(mesh):
    in_specs = (
        P("gy", "gx", None), P("gy", "gx"), P("gy", "gx", None, None),
        P(), P(), P(), P(), P(), P(),
    )
    out_specs = (P(), P("gy", "gx", None), P())
    return jax.shard_map(
        per_device, mesh=mesh, in_specs=in_specs, out_specs=out_specs, check_vma=False
    )
```

time: 83.7 us -> 69.8 us (0.83)
  Pallas kernels: 75.6 us -> 66.1 us
  local copies, waits for them, and re-layouts: 7.22 us -> 2.89 us
    pallas_call x1 -> x2, Pallas kernels: 75.6 us -> 66.1 us  [the longest x1 62 us: per_device(): pl.pallas_call(kernel, out_shape=(pltpu.VMEM((1, CH), F32), pltpu.VMEM((R...]
    unnamed x6, local copies, waits for them, and re-layouts: 7.22 us -> 2.89 us
where the time goes in v2:
time: 69.8 us; the launch traced here: 69.6 us
  Pallas kernels  66.1 us (95%)
  local copies, waits for them, and re-layouts  2.89 us (4%)
    pallas_call x1, Pallas kernels, per_device(): pl.pallas_call(kernel, out_shape=(pltpu.VMEM((1, CH), F32), pltpu.VMEM((R...  62 us
    pallas_call x1, Pallas kernels, per_device(): pl.pallas_call(finish, out_shape=(jax.ShapeDtypeStruct((1, CH), F32), jax...  4.05 us
    unnamed x6, local copies, waits for them, and re-layouts  2.89 us

profile of v2, /device:TPU:1, one launch (start us, length us, event | category | flops | bytes accessed | tf_op | source)
XLA Modules:
  0.0 69.6 jit_solution(11244622048304032511)
XLA Ops:
  0.6 62.0 %shard_map.112 = (f32[1,256]{1,0:T(1,128)S(1)}, bf16[32,128,256]{2,1,0:T(8,128)(2,1)S(1)}, bf16[2,2304,128]{2,1,0:T(8,128)(2,1)S(1)}) custom-call(bf16[32,128,256]{2,1,0:T(8,128)(2,1)} %feat.1, s32[2,8]{1,0:T(2,128)} %tissue.1, s32[1,16]{1,0:T(1,128)} %bitcast.9, bf16[3,768,256]{2,1,0:T(8,128)(2,1)} %bitcast.6, bf16[1024,256]{1,0:T(8,128)(2,1)} %bitcast.7, ...), custom_call_target="tpu_custom_call" | custom-call | tf_op jit(solution)/shard_map/pallas_call | solution.py:600
  62.7 0.0 copy-start
  62.7 1.3 %copy-done = bf16[32,128,256]{2,1,0:T(8,128)(2,1)} copy-done((bf16[32,128,256]{2,1,0:T(8,128)(2,1)}, bf16[32,128,256]{2,1,0:T(8,128)(2,1)S(1)}, u32[]{:S(2)}) %copy-start) | copy-done | bytes 2097176
  64.0 0.0 copy-start.1
  64.0 1.0 %copy-done.1 = bf16[2,2304,128]{2,1,0:T(8,128)(2,1)} copy-done((bf16[2,2304,128]{2,1,0:T(8,128)(2,1)}, bf16[2,2304,128]{2,1,0:T(8,128)(2,1)S(1)}, u32[]{:S(2)}) %copy-start.1) | copy-done | bytes 1179672
  65.0 0.0 copy-start.2
  65.0 0.5 copy-done.2
  65.6 4.0 %shard_map.113 = (f32[1,256]{1,0:T(1,128)}, bf16[32,128,256]{2,1,0:T(8,128)(2,1)}, f32[2304,256]{1,0:T(8,128)}) custom-call(f32[1,256]{1,0:T(1,128)} %copy-done.2, bf16[32,128,256]{2,1,0:T(8,128)(2,1)} %copy-done, bf16[2,2304,128]{2,1,0:T(8,128)(2,1)} %copy-done.1), custom_call_target="tpu_custom_call" | custom-call | tf_op jit(solution)/shard_map/pallas_call | solution.py:647
Async XLA Ops:
  62.7 1.3 %copy-start = (bf16[32,128,256]{2,1,0:T(8,128)(2,1)}, bf16[32,128,256]{2,1,0:T(8,128)(2,1)S(1)}, u32[]{:S(2)}) copy-start(bf16[32,128,256]{2,1,0:T(8,128)(2,1)S(1)} %get-tuple-element.10.grad) | copy-start | bytes 6291460
  64.0 1.0 %copy-start.1 = (bf16[2,2304,128]{2,1,0:T(8,128)(2,1)}, bf16[2,2304,128]{2,1,0:T(8,128)(2,1)S(1)}, u32[]{:S(2)}) copy-start(bf16[2,2304,128]{2,1,0:T(8,128)(2,1)S(1)} %get-tuple-element.11.conv) | copy-start | bytes 3538948
  65.0 0.5 copy-start.2

commit v3 on v2

--- a/solution.py
+++ b/solution.py
@@ -53,52 +53,55 @@
     emb_out, out_buf, full_w,
     field, cols3, trans, slope, grad3, taps, taps_t, stride_w, proj, parts3, mask,
     sums, spread, send_l, send_r, halo_l, halo_r, gsend_l, gsend_r, ghalo_l, ghalo_r,
-    edge_l, edge_r, tok_buf, code_rows, stride_back,
+    edge_l, edge_r, tok_buf, code_buf, code_rows, tissue_s, owner_s, cot_v, stride_back,
     local_w, pair_w, half_w, plane_w, line_w, emb_buf,
     load_sem, halo_ssem, halo_rsem, ghalo_ssem, ghalo_rsem, tok_ssem, tok_rsem,
     plane_ssem, plane_rsem, line_ssem, line_rsem, pair_ssem, pair_rsem, emb_ssem, emb_rsem,
 ):
     g, h = lax.axis_index("gy"), lax.axis_index("gx")
-    x_hi, y = g // 4, g % 4
-    z, x_lo, core = h // 4, (h // 2) % 2, h % 2
+    x_hi, y = lax.div(g, 4), lax.rem(g, 4)
+    z, x_lo, core = lax.div(h, 4), lax.rem(lax.div(h, 2), 2), lax.rem(h, 2)
     position = {"x": 2 * x_hi + x_lo, "y": y, "z": z}
     partner = (g, h + 1 - 2 * core)
 
-    def device_at(**moved):
-        spot = dict(position, **moved)
+    around = {axis: [lax.rem(position[axis] + j, 4) for j in range(4)] for axis in "xyz"}
+    share_g = {
+        "x": [lax.div(pos, 2) * 4 for pos in around["x"]],
+        "y": around["y"],
+        "z": [0] * 4,
+    }
+    share_h = {
+        "x": [lax.rem(pos, 2) * 2 for pos in around["x"]],
+        "y": [0] * 4,
+        "z": [pos * 4 for pos in around["z"]],
+    }
+
+    def device_at(**steps):
+        steps = {axis: steps.get(axis, 0) for axis in "xyz"}
         return (
-            (spot["x"] // 2) * 4 + spot["y"],
-            spot["z"] * 4 + (spot["x"] % 2) * 2 + core,
+            sum(share_g[axis][steps[axis]] for axis in "xy"),
+            sum(share_h[axis][steps[axis]] for axis in "xz") + core,
         )
 
-    def on_axis(axis, pos):
-        return device_at(**{axis: pos})
-
-    def on_plane(axes, member):
-        return device_at(**{axes[0]: member // 4, axes[1]: member % 4})
-
-    def member_of(axes):
-        return position[axes[0]] * 4 + position[axes[1]]
-
-    up, down = (g + GY - 1) % GY, (g + 1) % GY
-    left, right = (h + GX - 1) % GX, (h + 1) % GX
+    def plane_steps():
+        return [(j, k) for j in range(4) for k in range(4) if (j, k) != (0, 0)]
+
+    def on_plane(axes, j, k):
+        return device_at(**{axes[0]: j, axes[1]: k})
+
+    def member_of(axes, j=0, k=0):
+        return around[axes[0]][j] * 4 + around[axes[1]][k]
+
+    row_peers = [lax.rem(h + j, GX) for j in range(GX)]
+
+    up, down = lax.rem(g + GY - 1, GY), lax.rem(g + 1, GY)
+    left, right = row_peers[GX - 1], row_peers[1]
 
     def remote(src, dst, ssem, rsem, device):
         return pltpu.make_async_remote_copy(
             src_ref=src, dst_ref=dst, send_sem=ssem, recv_sem=rsem,
             device_id=device, device_id_type=MESH,
         )
-
-    barrier = pltpu.get_barrier_semaphore()
-    peers = [
-        (up, h), (down, h), (g, left), (g, right),
-        (up, left), (up, right), (down, left), (down, right),
-    ]
-    peers += [(g, (h + j) % GX) for j in range(1, GX)]
-    for axes in ("xy", "yz", "zx"):
-        peers += [on_plane(axes, (member_of(axes) + j) % 16) for j in range(1, 16)]
-    for device in peers:
-        pl.semaphore_signal(barrier, inc=1, device_id=device, device_id_type=MESH)
 
     loads = [
         pltpu.make_async_copy(feat, field.at[pl.ds(1, ROWS)], load_sem.at[0]),
@@ -108,14 +111,34 @@
         pltpu.make_async_copy(w_key, proj.at[:, pl.ds(CH, CH)], load_sem.at[4]),
         pltpu.make_async_copy(w_value, proj.at[:, pl.ds(2 * CH, CH)], load_sem.at[5]),
     ]
-    for copy in loads:
+    small = [
+        pltpu.make_async_copy(tissue, tissue_s, load_sem.at[6]),
+        pltpu.make_async_copy(owner, owner_s, load_sem.at[7]),
+        pltpu.make_async_copy(cot, cot_v, load_sem.at[8]),
+    ]
+    loads[0].start()
+    barrier = pltpu.get_barrier_semaphore()
+    peers = [
+        (up, h), (down, h), (g, left), (g, right),
+        (up, left), (up, right), (down, left), (down, right),
+    ]
+    peers += [(g, peer) for peer in row_peers[1:]]
+    for axes in ("xy", "yz", "zx"):
+        peers += [on_plane(axes, j, k) for j, k in plane_steps()]
+    for device in peers:
+        pl.semaphore_signal(barrier, inc=1, device_id=device, device_id_type=MESH)
+
+    for copy in loads[1:] + small:
         copy.start()
+    for copy in small:
+        copy.wait()
     for tile in range(TILES):
         tr, tc = tile // 8, tile % 8
-        flag = tissue[tr, tc].astype(F32)
-        code = flag * (owner[0, tile].astype(F32) + 1.0)
+        flag = tissue_s[tr, tc].astype(F32)
+        code = flag * (owner_s[0, tile].astype(F32) + 1.0)
         mask[tr, tc * 16 : tc * 16 + 16, :] = jnp.zeros((16, CH), F32) + flag
         code_rows[tile : tile + 1, :] = jnp.zeros((1, 128), F32) + code
+    code_buf[h] = code_rows[...].astype(BF16)
     sums[...] = jnp.zeros_like(sums)
     loads[0].wait()
 
@@ -140,6 +163,27 @@
 
     has_left, has_right = h > 0, h < GX - 1
     has_up, has_down = g > 0, g < GY - 1
+    to_send = (
+        has_up, has_down, has_left, has_right,
+        has_down & has_right, has_up & has_right, has_down & has_left, has_up & has_left,
+    )
+    to_receive = (
+        has_down, has_up, has_right, has_left,
+        has_up & has_left, has_down & has_left, has_up & has_right, has_down & has_right,
+    )
+
+    def start_halos(copies):
+        for copy, there in zip(copies, to_send):
+            pl.when(there)(copy.start)
+
+    def receive_halos(copies):
+        for copy, there in zip(copies, to_receive):
+            pl.when(there)(copy.wait_recv)
+
+    def drain_halos(copies):
+        for copy, there in zip(copies, to_send):
+            pl.when(there)(copy.wait_send)
+
 
     def columns_of(center, before, after):
         spot = iota(center.shape, 0)
@@ -187,11 +231,18 @@
 
     lax.fori_loop(1, 3, forward_block, 0)
     pl.semaphore_wait(barrier, BARRIER_SIGNALS)
+    code_copies = [
+        remote(
+            code_buf.at[h], code_buf.at[h], tok_ssem.at[0, j], tok_rsem.at[0, j], (g, row_peers[j])
+        )
+        for j in range(1, GX)
+    ]
     halos = halo_copies(
         field.at[1], field.at[ROWS], field.at[0], field.at[PAD - 1],
         send_l, send_r, halo_l, halo_r, halo_ssem, halo_rsem,
     )
-    for copy in halos:
+    start_halos(halos)
+    for copy in code_copies:
         copy.start()
     lax.fori_loop(3, 7, forward_block, 0)
 
@@ -208,8 +259,7 @@
         loads[k].wait()
     for k, part in enumerate(three_parts(proj[...])):
         parts3[k] = part
-    for copy in halos:
-        copy.wait_recv()
+    receive_halos(halos)
 
     def patch_row(row, carry):
         near = halo_l[pl.ds(7 + row, 1), :]
@@ -286,10 +336,11 @@
     normed = (pooled * inverse).astype(BF16)
 
     code = code_rows[...]
-    tok_buf[h, :, 0:CH] = normed
-    tok_buf[h, :, CH : CH + 128] = code.astype(BF16)
+    tok_buf[h] = normed
     tok_copies = [
-        remote(tok_buf.at[h], tok_buf.at[h], tok_ssem.at[j], tok_rsem.at[j], (g, (h + j) % GX))
+        remote(
+            tok_buf.at[h], tok_buf.at[h], tok_ssem.at[1, j], tok_rsem.at[1, j], (g, row_peers[j])
+        )
         for j in range(1, GX)
     ]
     for copy in tok_copies:
@@ -307,7 +358,7 @@
     own_qkv = sum(jnp.dot(normed, parts3[k], preferred_element_type=F32) for k in range(3))
     own_value = own_qkv[:, 2 * CH : 3 * CH]
     query_by_head, key_by_head = by_head(own_qkv[:, 0:CH]), by_head(own_qkv[:, CH : 2 * CH])
-    seed = cot[...] * (loss_scale / math.sqrt(GY * GX * TILES))
+    seed = cot_v[...] * (loss_scale / math.sqrt(GY * GX * TILES))
     seed_by_head = by_head(jnp.broadcast_to(seed, (8, CH)))
     value_seed = exact_dot(seed_by_head, proj[:, 2 * CH : 3 * CH], 1, 1)
     own_value_seed = jnp.sum(by_head(own_value * seed), axis=1, keepdims=True)
@@ -324,8 +375,10 @@
     for copy in tok_copies:
         copy.wait_recv()
 
-    everyone = tok_buf[:, :, 0:CH].reshape(GX * TILES, CH)
-    codes = tok_buf[:, :, CH : CH + 128].reshape(GX * TILES, 128)
+    everyone = tok_buf[...].reshape(GX * TILES, CH)
+    for copy in code_copies:
+        copy.wait_recv()
+    codes = code_buf[...].reshape(GX * TILES, 128)
     all_qk = sum(
         jnp.dot(everyone, parts3[k, :, 0 : 2 * CH], preferred_element_type=F32) for k in range(3)
     )
@@ -362,7 +415,7 @@
         axis, count, pos = emb_steps[step]
         copies = []
         for j in range(1, count):
-            device = partner if axis == "core" else on_axis(axis, (pos + j) % 4)
+            device = partner if axis == "core" else device_at(**{axis: j})
             spot = emb_buf.at[step, pos]
             copies.append(
                 remote(spot, spot, emb_ssem.at[step, j], emb_rsem.at[step, j], device)
@@ -412,8 +465,7 @@
         grad3.at[0, :, middle], grad3.at[PAD - 1, :, middle],
         gsend_l, gsend_r, ghalo_l, ghalo_r, ghalo_ssem, ghalo_rsem,
     )
-    for copy in ghalos:
-        copy.start()
+    start_halos(ghalos)
 
     def chunk_rows(k):
         first, count, _ = CHUNKS[k]
@@ -435,18 +487,17 @@
 
     def plane_copies(k, back):
         axes = CHUNKS[k][2]
-        me = member_of(axes)
         copies = []
-        for j in range(1, 16):
-            to = (me + j) % 16
+        for n, (j, i) in enumerate(plane_steps()):
             if back:
-                source = target = full_w.at[core, block_rows(k, me)]
+                source = target = full_w.at[core, block_rows(k, member_of(axes))]
             else:
-                source, target = half_w.at[block_rows(k, to)], plane_w.at[j - 1, shard_rows(k)]
+                source = half_w.at[block_rows(k, member_of(axes, j, i))]
+                target = plane_w.at[n, shard_rows(k)]
             copies.append(
                 remote(
-                    source, target, plane_ssem.at[back, k, j], plane_rsem.at[back, k, j],
-                    on_plane(axes, to),
+                    source, target, plane_ssem.at[back, k, n], plane_rsem.at[back, k, n],
+                    on_plane(axes, j, i),
                 )
             )
         return copies
@@ -457,7 +508,7 @@
         spot = line_w.at[pos, shard_rows(k)]
         return [
             remote(
-                spot, spot, line_ssem.at[k, j], line_rsem.at[k, j], on_axis(axis, (pos + j) % 4)
+                spot, spot, line_ssem.at[k, j], line_rsem.at[k, j], device_at(**{axis: j})
             )
             for j in range(1, 4)
         ]
@@ -520,8 +571,7 @@
         if k < 3:
             emb_start(k + 1, emb_finish(k))
 
-    for copy in ghalos:
-        copy.wait_recv()
+    receive_halos(ghalos)
 
     def grad_shift(row, carry):
         wide = grad3[row, :, CH : 2 * CH].astype(F32)
@@ -558,7 +608,9 @@
             if step > 3 or chunk > 1:
                 reduce_step(chunk, step)
 
-    for copy in halos + ghalos + tok_copies:
+    drain_halos(halos)
+    drain_halos(ghalos)
+    for copy in code_copies + tok_copies:
         copy.wait_send()
     for k in range(len(CHUNKS)):
         for copy in [pair_copy(k), last_copy(k)] + line_copies(k):
@@ -592,7 +644,6 @@
 
 def per_device(features, tissue, owner_map, w_conv, w_stride, w_query, w_key, w_value, cotangent):
     whole = pl.BlockSpec(memory_space=pl.ANY)
-    scalars = pl.BlockSpec(memory_space=pltpu.SMEM)
     vector = pl.BlockSpec(memory_space=pltpu.VMEM)
     dma = pltpu.SemaphoreType.DMA
     columns = pltpu.VMEM((ROWS, CH), F32)
@@ -604,7 +655,7 @@
             pltpu.VMEM((ROWS, COLS, CH), BF16),
             pltpu.VMEM((2, 9 * CH, 128), BF16),
         ),
-        in_specs=[whole, scalars, scalars, whole, whole, whole, whole, whole, vector],
+        in_specs=[whole] * 9,
         out_specs=(vector, vector, vector),
         scratch_shapes=[
             pltpu.VMEM((PAD, COLS, CH), BF16),
@@ -623,8 +674,12 @@
             columns, columns, column_halo, column_halo,
             columns, columns, column_halo, column_halo,
             columns, columns,
-            pltpu.VMEM((GX, TILES, CH + 128), BF16),
+            pltpu.VMEM((GX, TILES, CH), BF16),
+            pltpu.VMEM((GX, TILES, 128), BF16),
             pltpu.VMEM((TILES, 128), F32),
+            pltpu.SMEM((2, 8), jnp.int32),
+            pltpu.SMEM((1, TILES), jnp.int32),
+            pltpu.VMEM((1, CH), F32),
             pltpu.VMEM((TILES, 4 * CH), F32),
             pltpu.VMEM((2, 9 * CH, 128), BF16),
             pltpu.VMEM((9 * CH, 128), BF16),
@@ -632,8 +687,8 @@
             pltpu.VMEM((15, 144, 128), BF16),
             pltpu.VMEM((4, 144, 128), BF16),
             pltpu.VMEM((4, 4, 8, CH), F32),
-            dma((6,)), dma((8,)), dma((8,)), dma((8,)), dma((8,)),
-            dma((GX,)), dma((GX,)),
+            dma((9,)), dma((8,)), dma((8,)), dma((8,)), dma((8,)),
+            dma((2, GX)), dma((2, GX)),
             dma((2, 4, 16)), dma((2, 4, 16)), dma((4, 4)), dma((4, 4)), dma((2, 4)), dma((2, 4)),
             dma((4, 4)), dma((4, 4)),
         ],
@@ -654,7 +709,7 @@
         in_specs=[vector, vector, vector],
         out_specs=(whole, whole, whole),
         scratch_shapes=[pltpu.VMEM((9 * CH, CH), F32), dma((6,))],
-    )(embedding, input_grad, conv_grad)
+    )(*(pltpu.with_memory_space_constraint(x, pltpu.VMEM) for x in (embedding, input_grad, conv_grad)))
     return embedding.reshape(CH), input_grad, conv_grad.reshape(9, CH, CH)
 
 

time: 69.8 us -> 62.4 us (0.89)
  Pallas kernels: 66.1 us -> 61.6 us
  local copies, waits for them, and re-layouts: 2.89 us -> 0 us
    unnamed x6 -> x0, local copies, waits for them, and re-layouts: 2.89 us -> none
    pallas_call x1, Pallas kernels: 62 us -> 59.5 us  [per_device(): pl.pallas_call(kernel, out_shape=(pltpu.VMEM((1, CH), F32), pltpu.VMEM((R...]
    pallas_call x1, Pallas kernels: 4.05 us -> 2.15 us  [per_device(): pl.pallas_call(finish, out_shape=(jax.ShapeDtypeStruct((1, CH), F32), jax...]
where the time goes in v3:
time: 62.4 us; the launch traced here: 62.3 us
  Pallas kernels  61.6 us (99%)
  between operations  0.64 us (1%)
    pallas_call x1, Pallas kernels, per_device(): pl.pallas_call(kernel, out_shape=(pltpu.VMEM((1, CH), F32), pltpu.VMEM((R...  59.5 us
    pallas_call x1, Pallas kernels, per_device(): pl.pallas_call(finish, out_shape=(jax.ShapeDtypeStruct((1, CH), F32), jax...  2.15 us

profile of v3, /device:TPU:1, one launch (start us, length us, event | category | flops | bytes accessed | tf_op | source)
XLA Modules:
  0.0 62.3 jit_solution(13548470614135349047)
XLA Ops:
  0.6 59.5 %shard_map.112 = (f32[1,256]{1,0:T(1,128)S(1)}, bf16[32,128,256]{2,1,0:T(8,128)(2,1)S(1)}, bf16[2,2304,128]{2,1,0:T(8,128)(2,1)S(1)}) custom-call(bf16[32,128,256]{2,1,0:T(8,128)(2,1)} %feat.1, s32[2,8]{1,0:T(2,128)} %tissue.1, s32[1,16]{1,0:T(1,128)} %bitcast.9, bf16[3,768,256]{2,1,0:T(8,128)(2,1)} %bitcast.6, bf16[1024,256]{1,0:T(8,128)(2,1)} %bitcast.7, ...), custom_call_target="tpu_custom_call" | custom-call | tf_op jit(solution)/shard_map/pallas_call | solution.py:651
  60.1 2.1 %shard_map.113 = (f32[1,256]{1,0:T(1,128)}, bf16[32,128,256]{2,1,0:T(8,128)(2,1)}, f32[2304,256]{1,0:T(8,128)}) custom-call(f32[1,256]{1,0:T(1,128)S(1)} %get-tuple-element.9.emb, bf16[32,128,256]{2,1,0:T(8,128)(2,1)S(1)} %get-tuple-element.10.grad, bf16[2,2304,128]{2,1,0:T(8,128)(2,1)S(1)} %get-tuple-element.11.conv), custom_call_target="tpu_custom_call" | custom-call | tf_op jit(solution)/shard_map/pallas_call | solution.py:702

commit v4 on v3

--- a/solution.py
+++ b/solution.py
@@ -18,7 +18,7 @@
 PAD = ROWS + 2
 TILES = 16
 CONV_ROWS = 4
-CHUNKS = ((0, 3, "xyz"), (3, 3, "yzx"), (6, 2, "zxy"), (8, 1, "xyz"))
+CHUNKS = ((0, 3, "xyz"), (3, 3, "yzx"), (6, 3, "zxy"))
 BARRIER_SIGNALS = 23 + 15 * 3
 
 
@@ -27,6 +27,13 @@
         a, b, (((a_dim,), (b_dim,)), ((), ())),
         precision=lax.Precision.HIGHEST, preferred_element_type=F32,
     )
+
+
+def close_dot(a, b, a_dim=1, b_dim=0):
+    (a_high, a_low, _), (b_high, b_low, _) = three_parts(a), three_parts(b)
+    rows = a.shape[0]
+    both = half_dot(jnp.concatenate([a_high, a_low], axis=0), b_high, a_dim, b_dim)
+    return both[:rows] + both[rows:] + half_dot(a_high, b_low, a_dim, b_dim)
 
 
 def half_dot(a, b, a_dim=1, b_dim=0):
@@ -176,8 +183,8 @@
         for copy, there in zip(copies, to_send):
             pl.when(there)(copy.start)
 
-    def receive_halos(copies):
-        for copy, there in zip(copies, to_receive):
+    def receive_halos(copies, first=0, last=8):
+        for copy, there in list(zip(copies, to_receive))[first:last]:
             pl.when(there)(copy.wait_recv)
 
     def drain_halos(copies):
@@ -229,7 +236,7 @@
             sums[tr, a] = total
         return carry
 
-    lax.fori_loop(1, 3, forward_block, 0)
+    lax.fori_loop(1, 5, forward_block, 0)
     pl.semaphore_wait(barrier, BARRIER_SIGNALS)
     code_copies = [
         remote(
@@ -242,53 +249,33 @@
         send_l, send_r, halo_l, halo_r, halo_ssem, halo_rsem,
     )
     start_halos(halos)
-    for copy in code_copies:
-        copy.start()
-    lax.fori_loop(3, 7, forward_block, 0)
-
-    def transpose_middle(row, carry):
-        lanes = pl.ds(pl.multiple_of(row * COLS, COLS), COLS)
-        trans[1, :, lanes] = cols3[row, :, CH : 2 * CH].T
-        return carry
-
-    lax.fori_loop(1, ROWS + 1, transpose_middle, 0)
-    for a in range(3):
-        for b in range(3):
-            taps_t[a, b * CH : (b + 1) * CH, :] = taps[a, b * CH : (b + 1) * CH, :].T
+    lax.fori_loop(5, 7, forward_block, 0)
+
     for k in range(3, 6):
         loads[k].wait()
     for k, part in enumerate(three_parts(proj[...])):
         parts3[k] = part
-    receive_halos(halos)
-
-    def patch_row(row, carry):
-        near = halo_l[pl.ds(7 + row, 1), :]
-        far = halo_r[pl.ds(7 + row, 1), :]
-        near = jnp.where(has_left, near, 0.0)
-        far = jnp.where(has_right, far, 0.0)
-        head = cols3[row, 0:16, 0:CH].astype(F32)
-        tail = cols3[row, COLS - 16 : COLS, 2 * CH : 3 * CH].astype(F32)
-        spot = iota(head.shape, 0)
-        cols3[row, 0:16, 0:CH] = jnp.where(spot == 0, near, head).astype(BF16)
-        cols3[row, COLS - 16 : COLS, 2 * CH : 3 * CH] = jnp.where(spot == 15, far, tail).astype(BF16)
-        return carry
-
-    lax.fori_loop(1, ROWS + 1, patch_row, 0)
+    receive_halos(halos, 0, 2)
     for row, present in ((0, has_up), (PAD - 1, has_down)):
         wide = jnp.where(present, field[row].astype(F32), 0.0)
-        near = jnp.where(has_left & present, halo_l[7 + row : 8 + row, :], 0.0)
-        far = jnp.where(has_right & present, halo_r[7 + row : 8 + row, :], 0.0)
-        low, high = columns_of(wide, near, far)
+        low, high = columns_of(wide, 0.0, 0.0)
         cols3[row, :, 0:CH] = low.astype(BF16)
         cols3[row, :, CH : 2 * CH] = wide.astype(BF16)
         cols3[row, :, 2 * CH : 3 * CH] = high.astype(BF16)
 
+    for copy in code_copies:
+        copy.start()
+
     lax.fori_loop(0, 2, lambda i, carry: forward_block(i * 7, carry), 0)
+    receive_halos(halos, 2)
     row_of = iota((ROWS, CH), 0)
-    inner_row = (row_of >= CONV_ROWS) & (row_of < ROWS - CONV_ROWS)
+    inside = ((row_of > 0) | has_up, None, (row_of < ROWS - 1) | has_down)
 
     def fix_edge(got, present, edge, own, tap_at, col):
-        terms = [jnp.where(present, got[7 + a : 7 + a + ROWS, :], 0.0).astype(BF16) for a in range(3)]
+        terms = []
+        for a in range(3):
+            there = present if inside[a] is None else inside[a] & present
+            terms.append(jnp.where(there, got[7 + a : 7 + a + ROWS, :], 0.0).astype(BF16))
         pre = edge[...]
         flag = jnp.where(row_of < 16, mask[0, col : col + 1, :], mask[1, col : col + 1, :])
         old = (own[...] + pre * jax.nn.sigmoid(pre) * flag).astype(BF16).astype(F32)
@@ -299,14 +286,14 @@
         gate = jax.nn.sigmoid(pre)
         new = (own[...] + pre * gate * flag).astype(BF16).astype(F32)
         slant = gate * (1.0 + pre * (1.0 - gate))
-        change = jnp.where(inner_row, new - old, 0.0)
+        change = new - old
         for tr in range(2):
             for a in range(2):
                 part = jnp.where((row_of // 16 == tr) & (row_of % 2 == a), change, 0.0)
                 sums[tr, a, col : col + 1, :] = sums[tr, a, col : col + 1, :] + jnp.sum(
                     part, axis=0, keepdims=True
                 )
-        for row in range(CONV_ROWS, ROWS - CONV_ROWS):
+        for row in range(ROWS):
             slope[row, col : col + 1, :] = slant[row : row + 1, :]
 
     fix_edge(halo_l, has_left, edge_l, send_l, 0, 0)
@@ -341,7 +328,7 @@
         remote(
             tok_buf.at[h], tok_buf.at[h], tok_ssem.at[1, j], tok_rsem.at[1, j], (g, row_peers[j])
         )
-        for j in range(1, GX)
+        for j in sorted(range(1, GX), key=lambda j: abs(j - GX // 2))
     ]
     for copy in tok_copies:
         copy.start()
@@ -363,15 +350,28 @@
     value_seed = exact_dot(seed_by_head, proj[:, 2 * CH : 3 * CH], 1, 1)
     own_value_seed = jnp.sum(by_head(own_value * seed), axis=1, keepdims=True)
 
+    def patch_row(row, carry):
+        near = halo_l[pl.ds(7 + row, 1), :]
+        far = halo_r[pl.ds(7 + row, 1), :]
+        there = ((row > 0) | has_up) & ((row < PAD - 1) | has_down)
+        near = jnp.where(has_left & there, near, 0.0)
+        far = jnp.where(has_right & there, far, 0.0)
+        head = cols3[row, 0:16, 0:CH].astype(F32)
+        tail = cols3[row, COLS - 16 : COLS, 2 * CH : 3 * CH].astype(F32)
+        spot = iota(head.shape, 0)
+        cols3[row, 0:16, 0:CH] = jnp.where(spot == 0, near, head).astype(BF16)
+        cols3[row, COLS - 16 : COLS, 2 * CH : 3 * CH] = jnp.where(spot == 15, far, tail).astype(BF16)
+        return carry
+
+    lax.fori_loop(0, PAD, patch_row, 0)
+
     def transpose_row(row, carry):
         lanes = pl.ds(pl.multiple_of(row * COLS, COLS), COLS)
-        for b in (0, 2):
+        for b in range(3):
             trans[b, :, lanes] = cols3[row, :, b * CH : (b + 1) * CH].T
         return carry
 
     lax.fori_loop(0, PAD, transpose_row, 0)
-    for row in (0, PAD - 1):
-        trans[1, :, row * COLS : (row + 1) * COLS] = cols3[row, :, CH : 2 * CH].T
     for copy in tok_copies:
         copy.wait_recv()
 
@@ -388,8 +388,8 @@
     allowed = ((codes_across == code[:, 0:1]) & (codes_across > 0.5)).astype(F32)
     allowed = jnp.concatenate([allowed] * HEADS, axis=0)
     scale = 1.0 / math.sqrt(CH // HEADS)
-    as_query = jax.nn.sigmoid(exact_dot(query_by_head, all_key, 1, 1) * scale + attention_bias)
-    as_key = jax.nn.sigmoid(exact_dot(key_by_head, all_query, 1, 1) * scale + attention_bias)
+    as_query = jax.nn.sigmoid(close_dot(query_by_head, all_key, 1, 1) * scale + attention_bias)
+    as_key = jax.nn.sigmoid(close_dot(key_by_head, all_query, 1, 1) * scale + attention_bias)
     weight_sums = jnp.sum(as_key * allowed, axis=1, keepdims=True)
     head_sums = join_heads(jnp.broadcast_to(weight_sums, (HEADS * TILES, CH)))
     partial = jnp.sum(head_sums * own_value, axis=0, keepdims=True)
@@ -398,8 +398,8 @@
     across = jnp.concatenate([across[8 * k : 8 * k + 8, :] for k in range(HEADS) for _ in range(2)], axis=0)
     d_as_query = across * allowed * as_query * (1.0 - as_query) * scale
     d_as_key = own_value_seed * allowed * as_key * (1.0 - as_key) * scale
-    d_query = join_heads(exact_dot(d_as_query, all_key))
-    d_key = join_heads(exact_dot(d_as_key, all_query))
+    d_query = join_heads(close_dot(d_as_query, all_key))
+    d_key = join_heads(close_dot(d_as_key, all_query))
     d_qkv = three_parts(jnp.concatenate([d_query, d_key, d_value], axis=1))
     d_tokens = jnp.zeros((TILES, CH), F32)
     for k in range(3):
@@ -563,12 +563,12 @@
             local_w[c, rows, :] = part[:, c * 128 : c * 128 + 128].astype(BF16)
         return carry
 
-    after_taps = [[(0, 0)], [(1, 0), (0, 1)], [(2, 0), (1, 1)], [(3, 0), (2, 1)]]
+    after_taps = [[(0, 0)], [(1, 0), (0, 1)], [(2, 0), (1, 1)]]
     for k, (first, count, _) in enumerate(CHUNKS):
         lax.fori_loop(first, first + count, tap_of, 0)
         for chunk, step in after_taps[k]:
             reduce_step(chunk, step)
-        if k < 3:
+        if k < 2:
             emb_start(k + 1, emb_finish(k))
 
     receive_halos(ghalos)
@@ -582,8 +582,11 @@
         grad3[row, :, 2 * CH : 3 * CH] = low.astype(BF16)
         return carry
 
+    for a in range(3):
+        for b in range(3):
+            taps_t[a, b * CH : (b + 1) * CH, :] = taps[a, b * CH : (b + 1) * CH, :].T
     lax.fori_loop(0, PAD // 2, grad_shift, 0)
-    reduce_step(3, 1)
+    reduce_step(2, 1)
     lax.fori_loop(PAD // 2, PAD, grad_shift, 0)
     for row, present in ((0, has_up), (PAD - 1, has_down)):
         edge = grad3[row].astype(F32)
@@ -597,16 +600,15 @@
             out_buf[first + k] = (total[k] + spread[tr, k % 2]).astype(BF16)
         return carry
 
-    order = [[(0, 2)], [(1, 2)], [(2, 2), (0, 3)], [(3, 2), (1, 3)]]
+    order = [[(0, 2)], [(1, 2)], [(0, 3), (2, 2)], [(1, 3)]]
     for part in range(4):
         for chunk, step in order[part]:
             reduce_step(chunk, step)
         lax.fori_loop(2 * part, 2 * part + 2, back_block, 0)
+    emb_start(3, emb_finish(2))
+    for chunk, step in [(2, 3), (0, 4), (1, 4), (2, 4), (0, 5), (1, 5), (2, 5)]:
+        reduce_step(chunk, step)
     emb_out[...] = emb_finish(3)[0:1, :] * (1.0 / math.sqrt(GY * GX * TILES))
-    for step in (3, 4, 5):
-        for chunk in range(4):
-            if step > 3 or chunk > 1:
-                reduce_step(chunk, step)
 
     drain_halos(halos)
     drain_halos(ghalos)
@@ -689,7 +691,7 @@
             pltpu.VMEM((4, 4, 8, CH), F32),
             dma((9,)), dma((8,)), dma((8,)), dma((8,)), dma((8,)),
             dma((2, GX)), dma((2, GX)),
-            dma((2, 4, 16)), dma((2, 4, 16)), dma((4, 4)), dma((4, 4)), dma((2, 4)), dma((2, 4)),
+            dma((2, 3, 16)), dma((2, 3, 16)), dma((3, 4)), dma((3, 4)), dma((2, 3)), dma((2, 3)),
             dma((4, 4)), dma((4, 4)),
         ],
         compiler_params=pltpu.CompilerParams(

time: 62.4 us -> 61.7 us (0.989)
    pallas_call x1, Pallas kernels: 59.5 us -> 58.8 us  [per_device(): pl.pallas_call(kernel, out_shape=(pltpu.VMEM((1, CH), F32), pltpu.VMEM((R...]
where the time goes in v4:
time: 61.7 us; the launch traced here: 61.6 us
  Pallas kernels  61 us (99%)
  between operations  0.64 us (1%)
    pallas_call x1, Pallas kernels, per_device(): pl.pallas_call(kernel, out_shape=(pltpu.VMEM((1, CH), F32), pltpu.VMEM((R...  58.8 us
    pallas_call x1, Pallas kernels, per_device(): pl.pallas_call(finish, out_shape=(jax.ShapeDtypeStruct((1, CH), F32), jax...  2.15 us

profile of v4, /device:TPU:1, one launch (start us, length us, event | category | flops | bytes accessed | tf_op | source)
XLA Modules:
  0.0 61.6 jit_solution(10487781337188565437)
XLA Ops:
  0.6 58.8 %shard_map.112 = (f32[1,256]{1,0:T(1,128)S(1)}, bf16[32,128,256]{2,1,0:T(8,128)(2,1)S(1)}, bf16[2,2304,128]{2,1,0:T(8,128)(2,1)S(1)}) custom-call(bf16[32,128,256]{2,1,0:T(8,128)(2,1)} %feat.1, s32[2,8]{1,0:T(2,128)} %tissue.1, s32[1,16]{1,0:T(1,128)} %bitcast.9, bf16[3,768,256]{2,1,0:T(8,128)(2,1)} %bitcast.6, bf16[1024,256]{1,0:T(8,128)(2,1)} %bitcast.7, ...), custom_call_target="tpu_custom_call" | custom-call | tf_op jit(solution)/shard_map/pallas_call | solution.py:653
  59.5 2.1 %shard_map.113 = (f32[1,256]{1,0:T(1,128)}, bf16[32,128,256]{2,1,0:T(8,128)(2,1)}, f32[2304,256]{1,0:T(8,128)}) custom-call(f32[1,256]{1,0:T(1,128)S(1)} %get-tuple-element.9.emb, bf16[32,128,256]{2,1,0:T(8,128)(2,1)S(1)} %get-tuple-element.10.grad, bf16[2,2304,128]{2,1,0:T(8,128)(2,1)S(1)} %get-tuple-element.11.conv), custom_call_target="tpu_custom_call" | custom-call | tf_op jit(solution)/shard_map/pallas_call | solution.py:704

commit v5 on v4

--- a/solution.py
+++ b/solution.py
@@ -18,8 +18,8 @@
 PAD = ROWS + 2
 TILES = 16
 CONV_ROWS = 4
-CHUNKS = ((0, 3, "xyz"), (3, 3, "yzx"), (6, 3, "zxy"))
-BARRIER_SIGNALS = 23 + 15 * 3
+CHUNKS = ((0, 3, "xyz"), (3, 3, "zxy"), (6, 3, "zxy"))
+BARRIER_SIGNALS = 23 + 24
 
 
 def exact_dot(a, b, a_dim=1, b_dim=0):
@@ -130,8 +130,11 @@
         (up, left), (up, right), (down, left), (down, right),
     ]
     peers += [(g, peer) for peer in row_peers[1:]]
-    for axes in ("xy", "yz", "zx"):
-        peers += [on_plane(axes, j, k) for j, k in plane_steps()]
+    peers += [
+        device_at(x=i, y=j, z=k)
+        for i in range(4) for j in range(4) for k in range(4)
+        if 0 in (j, k) and (i, j) != (0, 0)
+    ]
     for device in peers:
         pl.semaphore_signal(barrier, inc=1, device_id=device, device_id_type=MESH)
 

time: 61.7 us -> 61.2 us (level)
  no operation moved by 1% of the time
where the time goes in v5:
time: 61.2 us; the launch traced here: 61 us
  Pallas kernels  60.4 us (99%)
  between operations  0.64 us (1%)
    pallas_call x1, Pallas kernels, per_device(): pl.pallas_call(kernel, out_shape=(pltpu.VMEM((1, CH), F32), pltpu.VMEM((R...  58.3 us
    pallas_call x1, Pallas kernels, per_device(): pl.pallas_call(finish, out_shape=(jax.ShapeDtypeStruct((1, CH), F32), jax...  2.15 us

profile of v5, /device:TPU:1, one launch (start us, length us, event | category | flops | bytes accessed | tf_op | source)
XLA Modules:
  0.0 61.0 jit_solution(4985032615545902729)
XLA Ops:
  0.6 58.3 %shard_map.112 = (f32[1,256]{1,0:T(1,128)S(1)}, bf16[32,128,256]{2,1,0:T(8,128)(2,1)S(1)}, bf16[2,2304,128]{2,1,0:T(8,128)(2,1)S(1)}) custom-call(bf16[32,128,256]{2,1,0:T(8,128)(2,1)} %feat.1, s32[2,8]{1,0:T(2,128)} %tissue.1, s32[1,16]{1,0:T(1,128)} %bitcast.9, bf16[3,768,256]{2,1,0:T(8,128)(2,1)} %bitcast.6, bf16[1024,256]{1,0:T(8,128)(2,1)} %bitcast.7, ...), custom_call_target="tpu_custom_call" | custom-call | tf_op jit(solution)/shard_map/pallas_call | solution.py:656
  58.9 2.1 %shard_map.113 = (f32[1,256]{1,0:T(1,128)}, bf16[32,128,256]{2,1,0:T(8,128)(2,1)}, f32[2304,256]{1,0:T(8,128)}) custom-call(f32[1,256]{1,0:T(1,128)S(1)} %get-tuple-element.9.emb, bf16[32,128,256]{2,1,0:T(8,128)(2,1)S(1)} %get-tuple-element.10.grad, bf16[2,2304,128]{2,1,0:T(8,128)(2,1)S(1)} %get-tuple-element.11.conv), custom_call_target="tpu_custom_call" | custom-call | tf_op jit(solution)/shard_map/pallas_call | solution.py:707

commit v6 on v5

--- a/solution.py
+++ b/solution.py
@@ -18,7 +18,7 @@
 PAD = ROWS + 2
 TILES = 16
 CONV_ROWS = 4
-CHUNKS = ((0, 3, "xyz"), (3, 3, "zxy"), (6, 3, "zxy"))
+CHUNKS = ((0, 3, "zxy"), (3, 3, "zxy"), (6, 3, "zxy"))
 BARRIER_SIGNALS = 23 + 24
 
 

time: 61.2 us -> 61.1 us (level)
  no operation moved by 1% of the time
where the time goes in v6:
time: 61.1 us; the launch traced here: 61 us
  Pallas kernels  60.3 us (99%)
  between operations  0.64 us (1%)
    pallas_call x1, Pallas kernels, per_device(): pl.pallas_call(kernel, out_shape=(pltpu.VMEM((1, CH), F32), pltpu.VMEM((R...  58.2 us
    pallas_call x1, Pallas kernels, per_device(): pl.pallas_call(finish, out_shape=(jax.ShapeDtypeStruct((1, CH), F32), jax...  2.15 us

profile of v6, /device:TPU:1, one launch (start us, length us, event | category | flops | bytes accessed | tf_op | source)
XLA Modules:
  0.0 61.0 jit_solution(3448782051845552887)
XLA Ops:
  0.6 58.2 %shard_map.112 = (f32[1,256]{1,0:T(1,128)S(1)}, bf16[32,128,256]{2,1,0:T(8,128)(2,1)S(1)}, bf16[2,2304,128]{2,1,0:T(8,128)(2,1)S(1)}) custom-call(bf16[32,128,256]{2,1,0:T(8,128)(2,1)} %feat.1, s32[2,8]{1,0:T(2,128)} %tissue.1, s32[1,16]{1,0:T(1,128)} %bitcast.9, bf16[3,768,256]{2,1,0:T(8,128)(2,1)} %bitcast.6, bf16[1024,256]{1,0:T(8,128)(2,1)} %bitcast.7, ...), custom_call_target="tpu_custom_call" | custom-call | tf_op jit(solution)/shard_map/pallas_call | solution.py:656
  58.8 2.1 %shard_map.113 = (f32[1,256]{1,0:T(1,128)}, bf16[32,128,256]{2,1,0:T(8,128)(2,1)}, f32[2304,256]{1,0:T(8,128)}) custom-call(f32[1,256]{1,0:T(1,128)S(1)} %get-tuple-element.9.emb, bf16[32,128,256]{2,1,0:T(8,128)(2,1)S(1)} %get-tuple-element.10.grad, bf16[2,2304,128]{2,1,0:T(8,128)(2,1)S(1)} %get-tuple-element.11.conv), custom_call_target="tpu_custom_call" | custom-call | tf_op jit(solution)/shard_map/pallas_call | solution.py:707
